TPU v7x, 32 devices: a whole 2x2x4 slice. The times are simulated.
32 devices in a mesh: level: 4 (over y, x), basin: 8 (over z, core).
Axes of the slice: x: 2, y: 2, z: 4, core: 2. Of those that a mesh axis runs over, the one named last changes fastest.
Arguments:
- runoff: float32 [4, 64, 8192], P('level', None, 'basin'), may hold values from 0 to 0.1
- travel: float32 [4, 8192], P('level', 'basin'), may hold values from 1 to 8
- downstream: int32 [4, 8192], P('level', 'basin'), may hold values from -1 to 127, as said below
- inflow_src: int32 [4, 8192], P('level', 'basin'), may hold values from -1 to 63, as said below
- reach_unit: int32 [4, 8192], P('level', 'basin'), may hold values from 0 to 8191
- rates: float32 [2, 8192], P(None, ('level', 'basin')), may hold values from 0.02 to 1
- cotangent: float32 [4, 64, 8192], P('level', None, 'basin'), may hold values from -6 to 6
Outputs:
- flows: float32 [4, 64, 8192], P('level', None, 'basin')
- rate_grads: float32 [2, 8192], P(None, ('level', 'basin'))
Inputs may be any that keep to these rules, and one draw needn't show every extreme that they name: Each reach's downstream reach lies later in its own aligned block of 128 reaches, at most 8 positions on; the last reach of a block holds -1 and is the block's only outlet. `inflow_src`: in every level group each outlet number 0 to 63 is held by exactly one reach; every other reach holds -1.
All inputs are finite; a program needn't handle non-finite values.
Results may differ from a plain program's by a relative error of at most 0.00014.
Values sent between devices are 32-bit elements; how exact they have to be, the bound alone decides.
No kernel may reach another device: no remote copies, remote signals or barrier semaphores. Data moves between devices by JAX's collectives and lax.ppermute only.
A program may use at most 128 MiB of HBM per device.

v0:
```python
import jax
import jax.numpy as jnp
from jax import lax
from jax.experimental import pallas as pl
from jax.experimental.pallas import tpu as pltpu
from jax.sharding import PartitionSpec as P

BLK = 128
SPLIT_FAST = 0.6
MUSK_X = 0.2
LEVELS_AXES = ("level", "basin")
F32 = jnp.float32
BF16 = jnp.bfloat16
NN = (((1,), (0,)), ((), ()))
NT = (((1,), (1,)), ((), ()))
TN = (((0,), (0,)), ((), ()))
VMEM_LIMIT = 48 << 20


def mm(left, right, dims):
    return lax.dot_general(left, right, dims, preferred_element_type=F32)


def split2(value):
    high = value.astype(BF16)
    return high, (value - high.astype(F32)).astype(BF16)


def split3(value):
    high = value.astype(BF16)
    rest = value - high.astype(F32)
    mid = rest.astype(BF16)
    return high, mid, (rest - mid.astype(F32)).astype(BF16)


def mm3(left, right, dims):
    return (
        mm(left[0], right[0], dims) + mm(left[0], right[1], dims) + mm(left[1], right[0], dims)
    )


def pick(value, onehot, dims):
    high, mid, low = split3(value)
    return mm(high, onehot, dims) + mm(mid, onehot, dims) + mm(low, onehot, dims)


def pick_right(onehot, value, dims):
    high, mid, low = split3(value)
    return mm(onehot, high, dims) + mm(onehot, mid, dims) + mm(onehot, low, dims)


def iota(shape, axis):
    return lax.broadcasted_iota(jnp.int32, shape, axis)


def coefficients(travel):
    twokx = 2.0 * travel * MUSK_X
    denom = 2.0 * travel * (1.0 - MUSK_X) + 1.0
    coef_in = (1.0 - twokx) / denom
    coef_prev = (1.0 + twokx) / denom
    coef_keep = (2.0 * travel * (1.0 - MUSK_X) - 1.0) / denom
    return coef_in, coef_prev, coef_keep


def shift_up(value, steps):
    rows = value.shape[0]
    if steps % 8 == 0:
        return jnp.concatenate([value[steps:], jnp.zeros((steps, value.shape[1]), F32)], axis=0)
    moved = pltpu.roll(value, rows - steps, 0)
    return jnp.where(iota(value.shape, 0) < rows - steps, moved, 0.0)


def shift_down(value, steps):
    rows = value.shape[0]
    if steps % 8 == 0:
        return jnp.concatenate(
            [jnp.zeros((steps, value.shape[1]), F32), value[: rows - steps]], axis=0
        )
    moved = pltpu.roll(value, steps, 0)
    return jnp.where(iota(value.shape, 0) >= steps, moved, 0.0)


def blocks_kernel(travel_ref, down_ref, src_ref, cot_ref,
                  inv_ref, pow_ref, grad_ref, resp_ref, slot_ref, ids_ref):
    steps, reaches = cot_ref.shape
    blocks = reaches // BLK
    slots = slot_ref.shape[0]
    lanes = ids_ref.shape[1]
    coef_in, coef_prev, coef_keep = coefficients(travel_ref[...])
    eye_mask = iota((BLK, BLK), 0) == iota((BLK, BLK), 1)
    eye = eye_mask.astype(F32)
    each = range(blocks)

    def part(row, b):
        return row[:, b * BLK : (b + 1) * BLK]

    down = down_ref[...].astype(F32)
    downs = jnp.concatenate([part(down, b) for b in each], axis=0)
    columns = mm(eye.astype(BF16), downs.astype(BF16), NT)
    place = iota((BLK, BLK), 1).astype(F32)
    linked = [jnp.broadcast_to(columns[:, b : b + 1], (BLK, BLK)) == place for b in each]
    base = [jnp.where(linked[b], part(coef_in, b), 0.0) for b in each]
    mixing = [
        jnp.where(linked[b], part(coef_prev, b), 0.0) + jnp.where(eye_mask, part(coef_keep, b), 0.0)
        for b in each
    ]
    total = [eye + base[b] for b in each]
    halves = [split2(base[b]) for b in each]
    power = [mm3(halves[b], halves[b], NN) for b in each]
    for level in range(2, 8):
        last = level == 7
        for b in each:
            joined = total[b] if last else jnp.concatenate([power[b], total[b]], axis=1)
            if level <= 3:
                product = mm3(split2(power[b]), split2(joined), NN)
            else:
                product = mm(power[b].astype(BF16), joined.astype(BF16), NN)
            if last:
                total[b] = total[b] + product
            else:
                power[b] = product[:, :BLK]
                total[b] = total[b] + product[:, BLK:]
    inverse = [split2(total[b]) for b in each]
    for b in each:
        inv_ref[0, b] = inverse[b][0]
        inv_ref[1, b] = inverse[b][1]
    moves = [split2(mm3(split2(mixing[b]), inverse[b], NN)) for b in each]
    state = [cot_ref[:, b * BLK : (b + 1) * BLK] for b in each]
    unit = jnp.where((iota((8, BLK), 0) == 0) & (iota((8, BLK), 1) == BLK - 1), 1.0, 0.0)
    rows = [unit for b in each]
    count = steps.bit_length() - 1
    for level in range(count):
        size = 1 << level
        for b in each:
            pow_ref[level, 0, b] = moves[b][0]
            pow_ref[level, 1, b] = moves[b][1]
            keep = steps - size
            if size < 8:
                left = jnp.concatenate([shift_up(state[b], size), shift_down(rows[b], size)], axis=0)
                out = mm3(split2(left), moves[b], NT)
                state[b] = state[b] + out[:steps]
                rows[b] = rows[b] + out[steps:]
            else:
                left = jnp.concatenate([state[b][size:], rows[b]], axis=0)
                out = mm3(split2(left), moves[b], NT)
                state[b] = jnp.concatenate(
                    [state[b][:keep] + out[:keep], state[b][keep:]], axis=0
                )
                rows[b] = jnp.concatenate([rows[b], out[keep:]], axis=0)
        if level + 1 < count:
            moves = [split2(mm3(moves[b], moves[b], NN)) for b in each]
    chosen = (
        jnp.broadcast_to(src_ref[...], (lanes, reaches)) == iota((lanes, reaches), 0)
    ).astype(BF16)
    gathered = jnp.zeros((slots, 2 * steps), F32)
    for b in each:
        both = mm3(split2(jnp.concatenate([state[b], rows[b]], axis=0)), inverse[b], NT)
        grad = both[:steps]
        resp = both[steps:]
        grad_ref[:, b * BLK : (b + 1) * BLK] = grad
        resp_ref[b] = resp
        now = part(coef_in, b)
        before = part(coef_prev, b)
        sent = jnp.concatenate(
            [now * grad + before * shift_up(grad, 1), now * resp + before * shift_down(resp, 1)],
            axis=0,
        )
        gathered = gathered + pick_right(chosen[:slots, b * BLK : (b + 1) * BLK], sent, NT)
    slot_ref[...] = gathered
    numbers = (iota((8, reaches), 1) // BLK + 1).astype(BF16)
    ids_ref[...] = mm(numbers, chosen, NT)


def lag_sum(out_rows, weight_ref, level, padded_ref, forward):
    steps = out_rows
    total = jnp.zeros((steps, padded_ref.shape[1]), F32)
    for lag in range(steps):
        start = steps - lag if forward else lag
        total = total + weight_ref[level, lag : lag + 1, :] * padded_ref[start : start + steps, :]
    return total


def lookup_rows(unit, units_here, halves, width):
    lane = BLK
    owner = unit // units_here
    inside = unit - owner * units_here
    half = inside // lane
    low = inside - half * lane
    row = 8 * owner + half
    return row, row + halves, low


def grads_kernel(where_ref, got_ref, rain_ref, travel_ref, unit_ref, grad_ref, resp_ref,
                 send_ref, drive_ref, weight_ref, ids_ref,
                 lateral_ref, fast_ref, slow_ref, padded_ref, *, levels, basins, units_here):
    steps, reaches = rain_ref.shape
    blocks = reaches // BLK
    devices = levels * basins
    lanes = ids_ref.shape[2]
    outlets = basins * blocks
    halves = units_here // BLK
    level_id = where_ref[0]
    basin_id = where_ref[1]
    _, _, coef_keep = coefficients(travel_ref[...])
    fast_row, slow_row, low = lookup_rows(unit_ref[...], units_here, halves, reaches)
    places = (iota((BLK, reaches), 0) == jnp.broadcast_to(low, (BLK, reaches))).astype(BF16)
    table = got_ref[:, 8:16, :].reshape(devices * 8, BLK)
    spread = pick(table, places, NN)
    row_of = iota((devices * 8, reaches), 0)
    fast_at = row_of == fast_row
    slow_at = row_of == slow_row
    fast_rate = jnp.sum(jnp.where(fast_at, spread, 0.0), axis=0, keepdims=True)
    slow_rate = jnp.sum(jnp.where(slow_at, spread, 0.0), axis=0, keepdims=True)
    fast_keep = jnp.exp(-fast_rate)
    slow_keep = jnp.exp(-slow_rate)
    fast_in = (1.0 - fast_keep) * SPLIT_FAST
    slow_in = (1.0 - slow_keep) * (1.0 - SPLIT_FAST)
    zero = jnp.zeros((1, reaches), F32)
    fast, slow, fast_sens, slow_sens = zero, zero, zero, zero
    for step in range(steps):
        rain = rain_ref[step : step + 1, :]
        fast_sens = fast_keep * fast_sens + (fast - SPLIT_FAST * rain)
        slow_sens = slow_keep * slow_sens + (slow - (1.0 - SPLIT_FAST) * rain)
        fast = fast_keep * fast + fast_in * rain
        slow = slow_keep * slow + slow_in * rain
        lateral_ref[step : step + 1, :] = fast + slow
        fast_ref[step : step + 1, :] = fast_sens
        slow_ref[step : step + 1, :] = slow_sens
    drive = (1.0 - coef_keep) * lateral_ref[...]
    drive_ref[...] = drive
    local = []
    for b in range(blocks):
        padded = jnp.concatenate(
            [drive[:, b * BLK : (b + 1) * BLK], jnp.zeros((BLK - steps, BLK), F32)], axis=0
        )
        product = mm3(split2(resp_ref[b]), split2(padded), NT)
        skewed = pltpu.roll(product, 0, 1, stride=1, stride_axis=0)
        local.append(jnp.sum(skewed, axis=0, keepdims=True))
    padded_ref[steps:, :] = jnp.zeros((steps, lanes), F32)
    back = []
    for l in range(levels):
        first = l * basins
        data = got_ref[first : first + basins, 0:8, :].reshape(outlets, 2 * steps)
        if lanes > outlets:
            data = jnp.concatenate([data, jnp.zeros((lanes - outlets, 2 * steps), F32)], axis=0)
        turned = jnp.transpose(data)
        back.append(turned[:steps])
        weight_ref[l] = turned[steps:]
        number = jnp.zeros((1, lanes), F32)
        for d in range(basins):
            pieces = [
                got_ref[first + d, 8 + 2 * halves + k : 9 + 2 * halves + k, :]
                for k in range(lanes // BLK)
            ]
            row = pieces[0] if len(pieces) == 1 else jnp.concatenate(pieces, axis=1)
            number = number + jnp.where(row > 0.5, row + float(blocks * d), 0.0)
        ids_ref[l] = jnp.broadcast_to(number, (8, lanes))
    returned = back[levels - 1]
    mine = jnp.where(level_id == levels - 2, returned, 0.0)
    for l in range(levels - 2, 0, -1):
        member = (
            iota((lanes, lanes), 0).astype(F32) + 1.0
            == jnp.broadcast_to(ids_ref[l, 0:1, :], (lanes, lanes))
        ).astype(BF16)
        padded_ref[:steps, :] = pick(returned, member, NN)
        returned = back[l] + lag_sum(steps, weight_ref, l, padded_ref, False)
        mine = mine + jnp.where(level_id == l - 1, returned, 0.0)
    own = (iota((8, lanes), 1) == iota((8, lanes), 0) + basin_id * blocks).astype(BF16)
    if steps < BLK:
        mine = jnp.concatenate([mine, jnp.zeros((BLK - steps, lanes), F32)], axis=0)
    mine = pick_right(own, mine, NT)
    fast_sum = []
    slow_sum = []
    for b in range(blocks):
        spreadout = jnp.broadcast_to(mine[b : b + 1, :], (steps, BLK))
        at = iota((steps, BLK), 0)
        for bit in range(steps.bit_length() - 1):
            moved = pltpu.roll(spreadout, BLK - (1 << bit), 1)
            spreadout = jnp.where((at & (1 << bit)) != 0, moved, spreadout)
        resp = jnp.concatenate([resp_ref[b], jnp.zeros((BLK - steps, BLK), F32)], axis=0)
        grad = grad_ref[:, b * BLK : (b + 1) * BLK] + mm3(split2(spreadout), split2(resp), NN)
        side = slice(b * BLK, (b + 1) * BLK)
        fast_sum.append(jnp.sum(grad * fast_ref[:, side], axis=0, keepdims=True))
        slow_sum.append(jnp.sum(grad * slow_ref[:, side], axis=0, keepdims=True))
    scale = 1.0 - coef_keep
    fast_grad = -fast_keep * scale * jnp.concatenate(fast_sum, axis=1)
    slow_grad = -slow_keep * scale * jnp.concatenate(slow_sum, axis=1)
    terms = jnp.where(fast_at, fast_grad, 0.0) + jnp.where(slow_at, slow_grad, 0.0)
    send_ref[...] = pick(terms, places, NT).reshape(devices, 8, BLK)
    half = blocks // 2
    for i in range(half):
        pair = jnp.concatenate([local[i][:, :steps], local[i + half][:, :steps]], axis=1)
        send_ref[:, 8 - half + i, :] = jnp.broadcast_to(pair, (devices, BLK))


def flows_kernel(where_ref, got_ref, travel_ref, src_ref, drive_ref, weight_ref, ids_ref,
                 inv_ref, pow_ref, flow_ref, rate_ref, padded_ref, *, levels, basins):
    steps, reaches = drive_ref.shape
    blocks = reaches // BLK
    half = blocks // 2
    lanes = ids_ref.shape[2]
    level_id = where_ref[0]
    coef_in, coef_prev, _ = coefficients(travel_ref[...])
    rate_ref[...] = jnp.sum(got_ref[...], axis=0)
    padded_ref[:steps, :] = jnp.zeros((steps, lanes), F32)
    rows = basins * 8
    row = iota((rows, lanes), 0)
    column = iota((rows, lanes), 1)
    inner = row % 8
    left = ((inner >= 8 - half) & (column == (row // 8) * blocks + inner - (8 - half))).astype(BF16)
    right = ((inner >= 8 - half) & (column == (row // 8) * blocks + inner - (8 - half) + half)).astype(BF16)
    outlet = None
    chosen = jnp.zeros((steps, lanes), F32)
    for l in range(levels - 1):
        block = got_ref[l * basins : (l + 1) * basins].reshape(rows, BLK)
        block = jnp.where(iota((rows, BLK), 0) % 8 >= 8 - half, block, 0.0)
        local = pick(block, left, TN)[:steps] + pick(block, right, TN)[steps:]
        if l == 0:
            outlet = local
        else:
            padded_ref[steps:, :] = outlet
            arriving = lag_sum(steps, weight_ref, l, padded_ref, True)
            member = (
                iota((lanes, lanes), 0).astype(F32) + 1.0
                == jnp.broadcast_to(ids_ref[l, 0:1, :], (lanes, lanes))
            ).astype(BF16)
            outlet = local + pick(arriving, member, NT)
        chosen = chosen + jnp.where(level_id == l + 1, outlet, 0.0)
    source = (iota((lanes, reaches), 0) == jnp.broadcast_to(src_ref[...], (lanes, reaches))).astype(BF16)
    inflow = pick(chosen, source, NN)
    driving = coef_in * inflow + coef_prev * shift_down(inflow, 1) + drive_ref[...]
    each = range(blocks)
    state = [
        mm3(split2(driving[:, b * BLK : (b + 1) * BLK]), (inv_ref[0, b], inv_ref[1, b]), NN)
        for b in each
    ]
    for level in range(steps.bit_length() - 1):
        size = 1 << level
        for b in each:
            move = (pow_ref[level, 0, b], pow_ref[level, 1, b])
            if size < 8:
                state[b] = state[b] + mm3(split2(shift_down(state[b], size)), move, NN)
            else:
                out = mm3(split2(state[b][: steps - size]), move, NN)
                state[b] = jnp.concatenate([state[b][:size], state[b][size:] + out], axis=0)
    for b in each:
        flow_ref[:, b * BLK : (b + 1) * BLK] = state[b]


def per_device(runoff, travel, downstream, inflow_src, reach_unit, rates, cotangent):
    _, steps, reaches = runoff.shape
    blocks = reaches // BLK
    levels = lax.axis_size("level")
    basins = lax.axis_size("basin")
    devices = levels * basins
    outlets = basins * blocks
    lanes = -(-outlets // BLK) * BLK
    units_here = rates.shape[1]
    halves = units_here // BLK
    count = steps.bit_length() - 1
    shape = jax.ShapeDtypeStruct
    smem = pl.BlockSpec(memory_space=pltpu.SMEM)
    vmem = pl.BlockSpec(memory_space=pltpu.VMEM)
    params = pltpu.CompilerParams(vmem_limit_bytes=VMEM_LIMIT)
    where = jnp.stack([lax.axis_index("level"), lax.axis_index("basin")]).astype(jnp.int32)
    inverse, powers, grad, resp, slot, ids = pl.pallas_call(
        blocks_kernel,
        out_shape=(
            shape((2, blocks, BLK, BLK), BF16),
            shape((count, 2, blocks, BLK, BLK), BF16),
            shape((steps, reaches), F32),
            shape((blocks, steps, BLK), F32),
            shape((outlets, 2 * steps), F32),
            shape((8, lanes), F32),
        ),
        in_specs=[vmem] * 4,
        out_specs=(vmem,) * 6,
        compiler_params=params,
        name="blocks",
    )(travel, downstream, inflow_src, cotangent[0])
    parts = lax.all_to_all(slot.reshape(basins, blocks, 2 * steps), "basin", 0, 0)
    used = 2 * halves + lanes // BLK
    packet = jnp.concatenate(
        [
            jnp.sum(parts, axis=0),
            rates.reshape(2 * halves, BLK),
            ids[0].reshape(lanes // BLK, BLK),
            jnp.zeros((8 - used, BLK), F32),
        ],
        axis=0,
    )
    got = lax.all_to_all(jnp.broadcast_to(packet[None], (devices, 16, BLK)), LEVELS_AXES, 0, 0)
    sent, drive, weights, numbers = pl.pallas_call(
        lambda *refs: grads_kernel(*refs, levels=levels, basins=basins, units_here=units_here),
        out_shape=(
            shape((devices, 8, BLK), F32),
            shape((steps, reaches), F32),
            shape((levels, steps, lanes), F32),
            shape((levels, 8, lanes), F32),
        ),
        in_specs=[smem] + [vmem] * 6,
        out_specs=(vmem,) * 4,
        scratch_shapes=[pltpu.VMEM((steps, reaches), F32)] * 3 + [pltpu.VMEM((2 * steps, lanes), F32)],
        compiler_params=params,
        name="grads",
    )(where, got, runoff[0], travel, reach_unit, grad, resp)
    swapped = lax.all_to_all(sent, LEVELS_AXES, 0, 0)
    flows, totals = pl.pallas_call(
        lambda *refs: flows_kernel(*refs, levels=levels, basins=basins),
        out_shape=(shape((steps, reaches), F32), shape((8, BLK), F32)),
        in_specs=[smem] + [vmem] * 8,
        out_specs=(vmem,) * 2,
        scratch_shapes=[pltpu.VMEM((2 * steps, lanes), F32)],
        compiler_params=params,
        name="flows",
    )(where, swapped, travel, inflow_src, drive, weights, numbers, inverse, powers)
    return flows[None], totals[: 2 * halves].reshape(2, units_here)


def solution(mesh):
    placed = (
        P("level", None, "basin"),
        P("level", "basin"),
        P("level", "basin"),
        P("level", "basin"),
        P("level", "basin"),
        P(None, ("level", "basin")),
        P("level", None, "basin"),
    )
    return jax.shard_map(
        per_device,
        mesh=mesh,
        in_specs=placed,
        out_specs=(P("level", None, "basin"), P(None, ("level", "basin"))),
        check_vma=False,
    )
```

profile of v0, /device:TPU:0, one launch (start us, length us, event | category | flops | bytes accessed | tf_op | source)
XLA Modules:
  0.0 66.6 jit_solution(3112559839372526094)
XLA Ops:
  0.6 0.9 %copy-done.2 = f32[1,64,1024]{2,1,0:T(8,128)S(1)} copy-done((f32[1,64,1024]{2,1,0:T(8,128)S(1)}, f32[1,64,1024]{2,1,0:T(8,128)}, u32[]{:S(2)}) %copy-start.2) | copy-done | bytes 262168
  1.6 0.7 %copy-done.8 = f32[1,1024]{1,0:T(1,128)S(1)} copy-done((f32[1,1024]{1,0:T(1,128)S(1)}, f32[1,1024]{1,0:T(1,128)}, u32[]{:S(2)}) %copy-start.8) | copy-done | bytes 4120
  2.3 0.7 %copy-done.10 = s32[1,1024]{1,0:T(1,128)S(1)} copy-done((s32[1,1024]{1,0:T(1,128)S(1)}, s32[1,1024]{1,0:T(1,128)}, u32[]{:S(2)}) %copy-start.10) | copy-done | bytes 4120
  3.0 0.7 %copy-done.12 = s32[1,1024]{1,0:T(1,128)S(1)} copy-done((s32[1,1024]{1,0:T(1,128)S(1)}, s32[1,1024]{1,0:T(1,128)}, u32[]{:S(2)}) %copy-start.12) | copy-done | bytes 4120
  3.6 7.9 %blocks.1 = (bf16[2,8,128,128]{3,2,1,0:T(8,128)(2,1)S(1)}, bf16[6,2,8,128,128]{4,3,2,1,0:T(8,128)(2,1)S(1)}, f32[64,1024]{1,0:T(8,128)S(1)}, f32[8,64,128]{2,1,0...) custom-call(f32[1,1024]{1,0:T(1,128)S(1)} %copy-done.8, s32[1,1024]{1,0:T(1,128)S(1)} %copy-done.12, ...), custom_call_target="tpu_custom_call" | custom-call | tf_op jit(solution)/shard_map/blocks/pallas_call | solution.py:366
  11.5 0.8 %copy-done = bf16[2,8,128,128]{3,2,1,0:T(8,128)(2,1)} copy-done((bf16[2,8,128,128]{3,2,1,0:T(8,128)(2,1)}, bf16[2,8,128,128]{3,2,1,0:T(8,128)(2,1)S(1)}, u32[]{:S(2)}) %copy-start) | copy-done | bytes 524312
  12.3 0.7 %copy-done.4 = f32[64,1024]{1,0:T(8,128)} copy-done((f32[64,1024]{1,0:T(8,128)}, f32[64,1024]{1,0:T(8,128)S(1)}, u32[]{:S(2)}) %copy-start.4) | copy-done | bytes 262168
  13.0 0.7 %copy-done.6 = f32[8,64,128]{2,1,0:T(8,128)} copy-done((f32[8,64,128]{2,1,0:T(8,128)}, f32[8,64,128]{2,1,0:T(8,128)S(1)}, u32[]{:S(2)}) %copy-start.6) | copy-done | bytes 262168
  13.7 6.3 %all-to-all-start = ((f32[8,8,128]{2,1,0:T(8,128)}), f32[8,8,128]{2,1,0:T(8,128)S(1)}, u32[]{:S(2)}, u32[]{:S(2)}) async-start(f32[8,8,128]{2,1,0:T(8,128)} %bitcast.3), calls=%async_computation | async-start | bytes 65536 | tf_op jit(solution)/shard_map/all_to_all | solution.py:381
  20.0 0.7 %reshape.15 = f32[4,128]{1,0:T(4,128)S(1)} reshape(f32[2,256]{1,0:T(2,128)} %param.12) | data formatting | bytes 4096 | tf_op jit(solution)/shard_map/reshape | solution.py:386
  20.8 5.0 %all-to-all-done = f32[8,8,128]{2,1,0:T(8,128)S(1)} async-done(((f32[8,8,128]{2,1,0:T(8,128)}), f32[8,8,128]{2,1,0:T(8,128)S(1)}, u32[]{:S(2)}, u32[]{:S(2)}) %all-to-all-start) | async-done | bytes 32800 | tf_op jit(solution)/shard_map/all_to_all | solution.py:381
  25.9 0.7 %broadcast_in_dim.13 = f32[32,16,128]{2,1,0:T(8,128)} broadcast(f32[16,128]{1,0:T(8,128)S(1)} %maximum_maximum_fusion), dimensions={1,2} | broadcast | bytes 270336 | tf_op jit(solution)/shard_map/broadcast_in_dim | solution.py:392
  26.6 2.9 %all-to-all-start.1 = ((f32[32,16,128]{2,1,0:T(8,128)}), f32[32,16,128]{2,1,0:T(8,128)S(1)}, u32[]{:S(2)}, u32[]{:S(2)}) async-start(f32[32,16,128]{2,1,0:T(8,128)} %broadcast_in_dim.13), calls=%async_computation.1 | async-start | bytes 524288 | tf_op jit(solution)/shard_map/all_to_all | solution.py:392
  29.6 10.3 %all-to-all-done.1.refs_1_ = f32[32,16,128]{2,1,0:T(8,128)S(1)} async-done(((f32[32,16,128]{2,1,0:T(8,128)}), f32[32,16,128]{2,1,0:T(8,128)S(1)}, u32[]{:S(2)}, u32[]{:S(2)}) %all-to-all-start.1) | async-done | bytes 262176 | tf_op jit(solution)/shard_map/all_to_all | solution.py:392
  39.9 0.9 %copy-done.3 = f32[1,64,1024]{2,1,0:T(8,128)S(1)} copy-done((f32[1,64,1024]{2,1,0:T(8,128)S(1)}, f32[1,64,1024]{2,1,0:T(8,128)}, u32[]{:S(2)}) %copy-start.3) | copy-done | bytes 262168
  40.8 0.9 %copy-done.5 = f32[64,1024]{1,0:T(8,128)S(1)} copy-done((f32[64,1024]{1,0:T(8,128)S(1)}, f32[64,1024]{1,0:T(8,128)}, u32[]{:S(2)}) %copy-start.5) | copy-done | bytes 262168
  41.8 0.9 %copy-done.7 = f32[8,64,128]{2,1,0:T(8,128)S(1)} copy-done((f32[8,64,128]{2,1,0:T(8,128)S(1)}, f32[8,64,128]{2,1,0:T(8,128)}, u32[]{:S(2)}) %copy-start.7) | copy-done | bytes 262168
  42.7 0.7 %copy-done.9 = f32[1,1024]{1,0:T(1,128)S(1)} copy-done((f32[1,1024]{1,0:T(1,128)S(1)}, f32[1,1024]{1,0:T(1,128)}, u32[]{:S(2)}) %copy-start.9) | copy-done | bytes 4120
  43.4 0.7 %copy-done.13 = s32[1,1024]{1,0:T(1,128)S(1)} copy-done((s32[1,1024]{1,0:T(1,128)S(1)}, s32[1,1024]{1,0:T(1,128)}, u32[]{:S(2)}) %copy-start.13) | copy-done | bytes 4120
  44.1 5.5 %grads.1 = (f32[32,8,128]{2,1,0:T(8,128)S(1)}, f32[64,1024]{1,0:T(8,128)S(1)}, f32[4,64,128]{2,1,0:T(8,128)S(1)}, f32[4,8,128]{2,1,0:T(8,128)S(1)}) custom-call(s32[2]{0:T(128)S(1)} %pad_add_fusion.refs_0_, f32[32,16,128]{2,1,0:T(8,128)S(1)} %all-to-all-done.1.refs_1_, f32[64,1024]{1,0:T(8,128)S(1)} %bitcast.7, f32[1,1024]{1,0:T(1,128)S(1)} %copy-done.9, ...), custom_call_target="tpu_custom_call" | custom-call | tf_op jit(solution)/shard_map/grads/pallas_call | solution.py:393
  49.7 10.5 %all_to_all.15.refs_1_ = f32[32,8,128]{2,1,0:T(8,128)S(1)} all-to-all(f32[32,8,128]{2,1,0:T(8,128)S(1)} %get-tuple-element.18), channel_id=1, replica_groups=mesh['level'=4,'basin'=8] {'level','basin'}, dimensions={0} | all-to-all | bytes 262144 | tf_op jit(solution)/shard_map/all_to_all | solution.py:407
  60.2 1.0 %copy-done.1 = bf16[2,8,128,128]{3,2,1,0:T(8,128)(2,1)S(1)} copy-done((bf16[2,8,128,128]{3,2,1,0:T(8,128)(2,1)S(1)}, bf16[2,8,128,128]{3,2,1,0:T(8,128)(2,1)}, u32[]{:S(2)}) %copy-start.1) | copy-done | bytes 524312
  61.2 0.7 %copy-done.11 = s32[1,1024]{1,0:T(1,128)S(1)} copy-done((s32[1,1024]{1,0:T(1,128)S(1)}, s32[1,1024]{1,0:T(1,128)}, u32[]{:S(2)}) %copy-start.11) | copy-done | bytes 4120
  61.9 4.1 %flows.1 = (f32[64,1024]{1,0:T(8,128)}, f32[8,128]{1,0:T(8,128)S(1)}) custom-call(s32[2]{0:T(128)S(1)} %pad_add_fusion.refs_0_, f32[32,8,128]{2,1,0:T(8,128)S(1)} %all_to_all.15.refs_1_, f32[1,1024]{1,0:T(1,128)S(1)} %copy-done.9, s32[1,1024]{1,0:T(1,128)S(1)} %copy-done.11, f32[64,1024]{1,0:T(8,128)S(1)} %get-tuple-element.19.refs_4_, ...), custom_call_target="tpu_custom_call" | custom-call | tf_op jit(solution)/shard_map/flows/pallas_call | solution.py:408
  (22 shorter events, 0.9 us)
Async XLA Ops:
  0.6 1.0 %copy-start.2 = (f32[1,64,1024]{2,1,0:T(8,128)S(1)}, f32[1,64,1024]{2,1,0:T(8,128)}, u32[]{:S(2)}) copy-start(f32[1,64,1024]{2,1,0:T(8,128)} %param.13) | copy-start | bytes 786436
  1.6 0.7 %copy-start.8 = (f32[1,1024]{1,0:T(1,128)S(1)}, f32[1,1024]{1,0:T(1,128)}, u32[]{:S(2)}) copy-start(f32[1,1024]{1,0:T(1,128)} %refs_2_.1) | copy-start | bytes 12292
  2.3 0.7 %copy-start.10 = (s32[1,1024]{1,0:T(1,128)S(1)}, s32[1,1024]{1,0:T(1,128)}, u32[]{:S(2)}) copy-start(s32[1,1024]{1,0:T(1,128)} %refs_3_.3) | copy-start | bytes 12292
  3.0 0.7 %copy-start.12 = (s32[1,1024]{1,0:T(1,128)S(1)}, s32[1,1024]{1,0:T(1,128)}, u32[]{:S(2)}) copy-start(s32[1,1024]{1,0:T(1,128)} %down_ref.1) | copy-start | bytes 12292
  11.5 0.8 %copy-start = (bf16[2,8,128,128]{3,2,1,0:T(8,128)(2,1)}, bf16[2,8,128,128]{3,2,1,0:T(8,128)(2,1)S(1)}, u32[]{:S(2)}) copy-start(bf16[2,8,128,128]{3,2,1,0:T(8,128)(2,1)S(1)} %get-tuple-element.22.refs_7_) | copy-start | bytes 1572868
  12.3 0.7 %copy-start.4 = (f32[64,1024]{1,0:T(8,128)}, f32[64,1024]{1,0:T(8,128)S(1)}, u32[]{:S(2)}) copy-start(f32[64,1024]{1,0:T(8,128)S(1)} %get-tuple-element.16.refs_5_) | copy-start | bytes 786436
  13.0 0.7 %copy-start.6 = (f32[8,64,128]{2,1,0:T(8,128)}, f32[8,64,128]{2,1,0:T(8,128)S(1)}, u32[]{:S(2)}) copy-start(f32[8,64,128]{2,1,0:T(8,128)S(1)} %get-tuple-element.17.refs_6_) | copy-start | bytes 786436
  13.7 12.1 %all-to-all-start = ((f32[8,8,128]{2,1,0:T(8,128)}), f32[8,8,128]{2,1,0:T(8,128)S(1)}, u32[]{:S(2)}, u32[]{:S(2)}) async-start(f32[8,8,128]{2,1,0:T(8,128)} %bitcast.3), calls=%async_computation | async-start | bytes 65536 | tf_op jit(solution)/shard_map/all_to_all | solution.py:381
  26.6 13.3 %all-to-all-start.1 = ((f32[32,16,128]{2,1,0:T(8,128)}), f32[32,16,128]{2,1,0:T(8,128)S(1)}, u32[]{:S(2)}, u32[]{:S(2)}) async-start(f32[32,16,128]{2,1,0:T(8,128)} %broadcast_in_dim.13), calls=%async_computation.1 | async-start | bytes 524288 | tf_op jit(solution)/shard_map/all_to_all | solution.py:392
  39.9 1.0 %copy-start.3 = (f32[1,64,1024]{2,1,0:T(8,128)S(1)}, f32[1,64,1024]{2,1,0:T(8,128)}, u32[]{:S(2)}) copy-start(f32[1,64,1024]{2,1,0:T(8,128)} %param.7) | copy-start | bytes 786436
  40.8 0.9 %copy-start.5 = (f32[64,1024]{1,0:T(8,128)S(1)}, f32[64,1024]{1,0:T(8,128)}, u32[]{:S(2)}) copy-start(f32[64,1024]{1,0:T(8,128)} %copy-done.4) | copy-start | bytes 786436
  41.8 0.9 %copy-start.7 = (f32[8,64,128]{2,1,0:T(8,128)S(1)}, f32[8,64,128]{2,1,0:T(8,128)}, u32[]{:S(2)}) copy-start(f32[8,64,128]{2,1,0:T(8,128)} %copy-done.6) | copy-start | bytes 786436
  42.7 0.7 %copy-start.9 = (f32[1,1024]{1,0:T(1,128)S(1)}, f32[1,1024]{1,0:T(1,128)}, u32[]{:S(2)}) copy-start(f32[1,1024]{1,0:T(1,128)} %refs_2_.1) | copy-start | bytes 12292
  43.4 0.7 %copy-start.13 = (s32[1,1024]{1,0:T(1,128)S(1)}, s32[1,1024]{1,0:T(1,128)}, u32[]{:S(2)}) copy-start(s32[1,1024]{1,0:T(1,128)} %refs_4_.1) | copy-start | bytes 12292
  60.2 1.0 %copy-start.1 = (bf16[2,8,128,128]{3,2,1,0:T(8,128)(2,1)S(1)}, bf16[2,8,128,128]{3,2,1,0:T(8,128)(2,1)}, u32[]{:S(2)}) copy-start(bf16[2,8,128,128]{3,2,1,0:T(8,128)(2,1)} %copy-done) | copy-start | bytes 1572868
  61.2 0.7 %copy-start.11 = (s32[1,1024]{1,0:T(1,128)S(1)}, s32[1,1024]{1,0:T(1,128)}, u32[]{:S(2)}) copy-start(s32[1,1024]{1,0:T(1,128)} %refs_3_.3) | copy-start | bytes 12292
where the time goes:
time: 67.2 us; the launch traced here: 66.6 us
  Pallas kernels  17.5 us (26%)
  waiting for transfers between devices  15.3 us (23%)
  local copies, waits for them, and re-layouts  13.3 us (20%)
  blocking collectives  10.5 us (16%)
  starting transfers between devices  9.23 us (14%)
    unnamed x28, local copies, waits for them, and re-layouts  11.2 us
    all_to_all x1, blocking collectives, per_device(): swapped = lax.all_to_all(sent, LEVELS_AXES, 0, 0)  10.5 us
    all_to_all x1, waiting for transfers between devices, per_device(): lax.all_to_all(jnp.broadcast_to(packet[None], (devices, 16, BLK)), LEVELS...  10.3 us
    pallas_call x1, Pallas kernels, per_device(): pl.pallas_call(blocks_kernel, out_shape=(shape((2, blocks, BLK, BLK), BF1...  7.85 us
    all_to_all x1, starting transfers between devices, per_device(): lax.all_to_all(slot.reshape(basins, blocks, 2 * steps), 'basin', 0, 0)  6.33 us
    pallas_call x1, Pallas kernels, per_device(): pl.pallas_call(lambda *refs: grads_kernel(*refs, levels=levels, basins=ba...  5.55 us
    all_to_all x1, waiting for transfers between devices, per_device(): lax.all_to_all(slot.reshape(basins, blocks, 2 * steps), 'basin', 0, 0)  4.97 us
    pallas_call x1, Pallas kernels, per_device(): pl.pallas_call(lambda *refs: flows_kernel(*refs, levels=levels, basins=ba...  4.09 us
  transfers between devices with their start and end apart: 2, of which 2 were waited for; matrix products, arithmetic and copies ran while one was open for 1% of the time, Pallas kernels for 0%

commit v1 on v0

v1 whole, which is shorter than its diff:
```python
import jax
import jax.numpy as jnp
from jax import lax
from jax.experimental import pallas as pl
from jax.experimental.pallas import tpu as pltpu
from jax.sharding import PartitionSpec as P

BLK = 128
SPLIT_FAST = 0.6
MUSK_X = 0.2
LEVELS_AXES = ("level", "basin")
F32 = jnp.float32
BF16 = jnp.bfloat16
NN = (((1,), (0,)), ((), ()))
NT = (((1,), (1,)), ((), ()))
TN = (((0,), (0,)), ((), ()))
VMEM_LIMIT = 48 << 20
CAP = 16


def mm(left, right, dims):
    return lax.dot_general(left, right, dims, preferred_element_type=F32)


def split2(value):
    high = value.astype(BF16)
    return high, (value - high.astype(F32)).astype(BF16)


def split3(value):
    high = value.astype(BF16)
    rest = value - high.astype(F32)
    mid = rest.astype(BF16)
    return high, mid, (rest - mid.astype(F32)).astype(BF16)


def mm3(left, right, dims):
    return (
        mm(left[0], right[0], dims) + mm(left[0], right[1], dims) + mm(left[1], right[0], dims)
    )


def mm6(left, right, dims):
    small = mm(left[1], right[1], dims) + mm(left[0], right[2], dims) + mm(left[2], right[0], dims)
    return mm(left[0], right[0], dims) + (
        mm(left[0], right[1], dims) + mm(left[1], right[0], dims) + small
    )


def pick(value, onehot, dims):
    high, mid, low = split3(value)
    return mm(high, onehot, dims) + mm(mid, onehot, dims) + mm(low, onehot, dims)


def pick_right(onehot, value, dims):
    high, mid, low = split3(value)
    return mm(onehot, high, dims) + mm(onehot, mid, dims) + mm(onehot, low, dims)


def iota(shape, axis):
    return lax.broadcasted_iota(jnp.int32, shape, axis)


def coefficients(travel):
    twokx = 2.0 * travel * MUSK_X
    denom = 2.0 * travel * (1.0 - MUSK_X) + 1.0
    coef_in = (1.0 - twokx) / denom
    coef_prev = (1.0 + twokx) / denom
    coef_keep = (2.0 * travel * (1.0 - MUSK_X) - 1.0) / denom
    return coef_in, coef_prev, coef_keep


def shift_up(value, steps):
    rows = value.shape[0]
    if steps % 8 == 0:
        return jnp.concatenate([value[steps:], jnp.zeros((steps, value.shape[1]), F32)], axis=0)
    moved = pltpu.roll(value, rows - steps, 0)
    return jnp.where(iota(value.shape, 0) < rows - steps, moved, 0.0)


def shift_down(value, steps):
    rows = value.shape[0]
    if steps % 8 == 0:
        return jnp.concatenate(
            [jnp.zeros((steps, value.shape[1]), F32), value[: rows - steps]], axis=0
        )
    moved = pltpu.roll(value, steps, 0)
    return jnp.where(iota(value.shape, 0) >= steps, moved, 0.0)


def copies(pairs, sems):
    started = []
    for at, (source, target) in enumerate(pairs):
        copy = pltpu.make_async_copy(source, target, sems.at[at])
        copy.start()
        started.append(copy)
    return started


def stacked(row, blocks):
    return jnp.concatenate([row[:, b * BLK : (b + 1) * BLK] for b in range(blocks)], axis=0)


def blocks_kernel(where_ref, travel_hbm, down_hbm, src_hbm, rates_hbm, cot_hbm,
                  packet_ref, grad_hbm, resp_hbm, move_hbm,
                  travel_ref, down_ref, src_ref, rates_ref, cot_ref,
                  grad_ref, resp_ref, move_ref, in_sems, out_sems, *, basins):
    steps, reaches = cot_ref.shape
    blocks = reaches // BLK
    devices, height, _ = packet_ref.shape
    width = (height - CAP) // 8 * BLK
    each = range(blocks)
    loads = copies(
        [(travel_hbm, travel_ref), (down_hbm, down_ref), (src_hbm, src_ref),
         (rates_hbm, rates_ref), (cot_hbm.at[0], cot_ref)], in_sems
    )
    for copy in loads[:4]:
        copy.wait()
    coef_in, coef_prev, coef_keep = coefficients(travel_ref[...])
    eye_mask = iota((BLK, BLK), 0) == iota((BLK, BLK), 1)
    eye = eye_mask.astype(F32)

    def part(row, b):
        return row[:, b * BLK : (b + 1) * BLK]

    downs = stacked(down_ref[...].astype(F32), blocks)
    columns = mm(eye.astype(BF16), downs.astype(BF16), NT)
    place = iota((BLK, BLK), 1).astype(F32)
    turned = [
        pick_right(eye.astype(BF16), stacked(row, blocks), NT)
        for row in (coef_in, coef_prev, coef_keep)
    ]
    linked = [jnp.broadcast_to(columns[:, b : b + 1], (BLK, BLK)) == place for b in each]
    base = [jnp.where(linked[b], part(coef_in, b), 0.0) for b in each]
    hops = [linked[b].astype(BF16) for b in each]
    total = [eye + base[b] for b in each]
    power = base
    for level in range(1, 8):
        for b in each:
            if level == 1:
                joined = power[b]
            elif level == 7:
                joined = total[b]
            else:
                joined = jnp.concatenate([power[b], total[b]], axis=1)
            if level <= 3:
                scale = jnp.sum(power[b], axis=1, keepdims=True)
                product = scale * pick_right(hops[b], joined, NN)
            else:
                product = mm(power[b].astype(BF16), joined.astype(BF16), NN)
            if level <= 2:
                hops[b] = mm(hops[b], hops[b], NN).astype(BF16)
            if level == 1:
                power[b] = product
            elif level == 7:
                total[b] = total[b] + product
            else:
                power[b] = product[:, :BLK]
                total[b] = total[b] + product[:, BLK:]
    inverse = [split2(total[b]) for b in each]
    stores = []

    def publish(at, moves):
        for b in each:
            move_ref[at, 0, b] = moves[b][0]
            move_ref[at, 1, b] = moves[b][1]
        copy = pltpu.make_async_copy(move_ref.at[at], move_hbm.at[at], out_sems.at[at])
        copy.start()
        stores.append(copy)

    publish(0, inverse)
    following = [
        pick_right(linked[b].astype(BF16), turned[1][:, b : b + 1] * total[b], NN)
        + turned[2][:, b : b + 1] * total[b]
        for b in each
    ]
    moves = [split3(following[b]) for b in each]
    loads[4].wait()
    state = [cot_ref[:, b * BLK : (b + 1) * BLK] for b in each]
    unit = jnp.where((iota((8, BLK), 0) == 0) & (iota((8, BLK), 1) == BLK - 1), 1.0, 0.0)
    rows = [unit for b in each]
    count = steps.bit_length() - 1
    for level in range(count):
        size = 1 << level
        publish(level + 1, moves)
        keep = steps - size
        for b in each:
            if size < 8:
                left = jnp.concatenate([shift_up(state[b], size), shift_down(rows[b], size)], axis=0)
                out = mm3(split2(left), moves[b], NT)
                state[b] = state[b] + out[:steps]
                rows[b] = rows[b] + out[steps:]
            else:
                left = jnp.concatenate([state[b][size:], rows[b]], axis=0)
                out = mm3(split2(left), moves[b], NT)
                state[b] = jnp.concatenate(
                    [state[b][:keep] + out[:keep], state[b][keep:]], axis=0
                )
                rows[b] = jnp.concatenate([rows[b], out[keep:]], axis=0)
        if level + 1 < count:
            if level < 2:
                moves = [split3(mm6(moves[b], moves[b], NN)) for b in each]
            else:
                moves = [split2(mm3(moves[b], moves[b], NN)) for b in each]
    sources = stacked(src_ref[...], blocks)
    held = sources >= 0
    upper = (iota((BLK, BLK), 0) <= iota((BLK, BLK), 1)).astype(BF16)
    ranks = mm(held.astype(BF16), upper, NN)
    basin_id = where_ref[1]
    offset = jnp.zeros((1, 1), F32)
    packed = jnp.zeros((CAP, 2 * steps), F32)
    labels = jnp.zeros((8, width), F32)
    responses = []
    for b in each:
        both = mm3(split2(jnp.concatenate([state[b], rows[b]], axis=0)), inverse[b], NT)
        grad_ref[:, b * BLK : (b + 1) * BLK] = both[:steps]
        resp_ref[b] = both[steps:]
        responses.append(both)
    for copy in copies([(grad_ref, grad_hbm), (resp_ref, resp_hbm)], out_sems.at[pl.ds(count + 1, 2)]):
        stores.append(copy)
    for b in each:
        rank = jnp.where(held[b : b + 1], ranks[b : b + 1] + offset, 0.0)
        offset = offset + ranks[b : b + 1, BLK - 1 : BLK]
        row_at = iota((CAP, BLK), 0).astype(F32) + 1.0
        chosen = (jnp.broadcast_to(rank, (CAP, BLK)) == row_at).astype(BF16)
        grad = responses[b][:steps]
        resp = responses[b][steps:]
        now = part(coef_in, b)
        before = part(coef_prev, b)
        sent = jnp.concatenate(
            [now * grad + before * shift_up(grad, 1), now * resp + before * shift_down(resp, 1)],
            axis=0,
        )
        packed = packed + pick_right(chosen, sent, NT)
        lane_at = iota((width, BLK), 0) - basin_id * CAP
        wide = (
            (jnp.broadcast_to(rank, (width, BLK)) == lane_at.astype(F32) + 1.0) & (lane_at < CAP)
        ).astype(BF16)
        which = jnp.broadcast_to((sources[b : b + 1] + 1).astype(F32), (8, BLK))
        block_at = (basin_id * blocks + (b + 1)).astype(F32)
        values = jnp.where(iota((8, BLK), 0) == 0, which, block_at)
        labels = labels + mm(values.astype(BF16), wide, NT)
    labels = jnp.where(iota((8, width), 0) == 2, jnp.broadcast_to(offset, (8, width)), labels)
    parts = rates_ref.shape[1] // BLK
    rate_rows = [rates_ref[k : k + 1, h * BLK : (h + 1) * BLK] for k in range(2) for h in range(parts)]
    for group in range(width // BLK):
        rows_here = labels[:4, group * BLK : (group + 1) * BLK]
        first = CAP + 8 * group
        if group == 0:
            tail = rate_rows + [jnp.zeros((1, BLK), F32)] * (4 - len(rate_rows))
        else:
            tail = [jnp.zeros((4, BLK), F32)]
        piece = jnp.concatenate([rows_here] + tail, axis=0)
        packet_ref[:, first : first + 8, :] = jnp.broadcast_to(piece[None], (devices, 8, BLK))
    packet_ref[:, :CAP, :] = jnp.broadcast_to(packed[None], (devices, CAP, BLK))
    for copy in stores:
        copy.wait()


def lag_sum(out_rows, weight_ref, level, padded_ref, forward):
    steps = out_rows
    total = jnp.zeros((steps, padded_ref.shape[1]), F32)
    for lag in range(steps):
        start = steps - lag if forward else lag
        total = total + weight_ref[level, lag : lag + 1, :] * padded_ref[start : start + steps, :]
    return total


def lookup_rows(unit, units_here, halves, width):
    lane = BLK
    owner = unit // units_here
    inside = unit - owner * units_here
    half = inside // lane
    low = inside - half * lane
    row = 8 * owner + 4 + half
    return row, row + halves, low


def grads_kernel(where_ref, got_ref, travel_hbm, unit_hbm, rain_hbm, grad_hbm, resp_hbm,
                 send_ref, drive_ref, weight_ref, ids_ref, full_ref,
                 travel_ref, unit_ref, rain_ref, grad_ref, resp_ref,
                 lateral_ref, fast_ref, slow_ref, padded_ref, sems, *, levels, basins, units_here):
    steps, reaches = rain_ref.shape
    loads = copies(
        [(travel_hbm, travel_ref), (unit_hbm, unit_ref), (rain_hbm.at[0], rain_ref),
         (resp_hbm, resp_ref), (grad_hbm, grad_ref)], sems
    )
    blocks = reaches // BLK
    devices = levels * basins
    lanes = ids_ref.shape[2]
    full_ref[0] = jnp.max(got_ref[basins:, CAP + 2 : CAP + 3, :]).astype(jnp.int32)
    outlets = basins * blocks
    halves = units_here // BLK
    level_id = where_ref[0]
    basin_id = where_ref[1]
    padded_ref[steps:, :] = jnp.zeros((steps, lanes), F32)
    back = [None]
    for l in range(1, levels):
        first = l * basins
        data = got_ref[first : first + basins, :CAP, :].reshape(basins * CAP, BLK)
        turned = jnp.transpose(data)
        labels = jnp.concatenate(
            [
                jnp.sum(got_ref[first : first + basins, CAP + 8 * g : CAP + 8 * g + 8, :], axis=0)
                for g in range((got_ref.shape[1] - CAP) // 8)
            ],
            axis=1,
        )[:, : basins * CAP]
        slot_of = (
            jnp.broadcast_to(labels[0:1], (lanes, basins * CAP))
            == iota((lanes, basins * CAP), 0).astype(F32) + 1.0
        ).astype(BF16)
        dense = pick(turned, slot_of, NT)
        back.append(dense[:steps])
        weight_ref[l] = dense[steps:]
        ids_ref[l] = mm(labels.astype(BF16), slot_of, NT)
    returned = back[levels - 1]
    mine = jnp.where(level_id == levels - 2, returned, 0.0)
    for l in range(levels - 2, 0, -1):
        member = (
            iota((lanes, lanes), 0).astype(F32) + 1.0
            == jnp.broadcast_to(ids_ref[l, 1:2, :], (lanes, lanes))
        ).astype(BF16)
        padded_ref[:steps, :] = pick(returned, member, NN)
        returned = back[l] + lag_sum(steps, weight_ref, l, padded_ref, False)
        mine = mine + jnp.where(level_id == l - 1, returned, 0.0)
    own = (iota((8, lanes), 1) == iota((8, lanes), 0) + basin_id * blocks).astype(BF16)
    if steps < BLK:
        mine = jnp.concatenate([mine, jnp.zeros((BLK - steps, lanes), F32)], axis=0)
    mine = pick_right(own, mine, NT)
    loads[0].wait()
    loads[1].wait()
    _, _, coef_keep = coefficients(travel_ref[...])
    fast_row, slow_row, low = lookup_rows(unit_ref[...], units_here, halves, reaches)
    places = (iota((BLK, reaches), 0) == jnp.broadcast_to(low, (BLK, reaches))).astype(BF16)
    table = got_ref[:, CAP : CAP + 8, :].reshape(devices * 8, BLK)
    spread = pick(table, places, NN)
    row_of = iota((devices * 8, reaches), 0)
    fast_at = row_of == fast_row
    slow_at = row_of == slow_row
    fast_rate = jnp.sum(jnp.where(fast_at, spread, 0.0), axis=0, keepdims=True)
    slow_rate = jnp.sum(jnp.where(slow_at, spread, 0.0), axis=0, keepdims=True)
    fast_keep = jnp.exp(-fast_rate)
    slow_keep = jnp.exp(-slow_rate)
    fast_in = (1.0 - fast_keep) * SPLIT_FAST
    slow_in = (1.0 - slow_keep) * (1.0 - SPLIT_FAST)
    loads[2].wait()
    zero = jnp.zeros((1, reaches), F32)
    fast, slow, fast_sens, slow_sens = zero, zero, zero, zero
    for step in range(steps):
        rain = rain_ref[step : step + 1, :]
        fast_sens = fast_keep * fast_sens + (fast - SPLIT_FAST * rain)
        slow_sens = slow_keep * slow_sens + (slow - (1.0 - SPLIT_FAST) * rain)
        fast = fast_keep * fast + fast_in * rain
        slow = slow_keep * slow + slow_in * rain
        lateral_ref[step : step + 1, :] = fast + slow
        fast_ref[step : step + 1, :] = fast_sens
        slow_ref[step : step + 1, :] = slow_sens
    drive = (1.0 - coef_keep) * lateral_ref[...]
    drive_ref[...] = drive
    loads[3].wait()
    local = []
    for b in range(blocks):
        padded = jnp.concatenate(
            [drive[:, b * BLK : (b + 1) * BLK], jnp.zeros((BLK - steps, BLK), F32)], axis=0
        )
        product = mm3(split2(resp_ref[b]), split2(padded), NT)
        skewed = pltpu.roll(product, 0, 1, stride=1, stride_axis=0)
        local.append(jnp.sum(skewed, axis=0, keepdims=True))
    loads[4].wait()
    fast_sum = []
    slow_sum = []
    for b in range(blocks):
        spreadout = jnp.broadcast_to(mine[b : b + 1, :], (steps, BLK))
        at = iota((steps, BLK), 0)
        for bit in range(steps.bit_length() - 1):
            moved = pltpu.roll(spreadout, BLK - (1 << bit), 1)
            spreadout = jnp.where((at & (1 << bit)) != 0, moved, spreadout)
        resp = jnp.concatenate([resp_ref[b], jnp.zeros((BLK - steps, BLK), F32)], axis=0)
        grad = grad_ref[:, b * BLK : (b + 1) * BLK] + mm3(split2(spreadout), split2(resp), NN)
        side = slice(b * BLK, (b + 1) * BLK)
        fast_sum.append(jnp.sum(grad * fast_ref[:, side], axis=0, keepdims=True))
        slow_sum.append(jnp.sum(grad * slow_ref[:, side], axis=0, keepdims=True))
    scale = 1.0 - coef_keep
    fast_grad = -fast_keep * scale * jnp.concatenate(fast_sum, axis=1)
    slow_grad = -slow_keep * scale * jnp.concatenate(slow_sum, axis=1)
    terms = jnp.where(fast_at, fast_grad, 0.0) + jnp.where(slow_at, slow_grad, 0.0)
    send_ref[...] = pick(terms, places, NT).reshape(devices, 8, BLK)
    half = blocks // 2
    for i in range(half):
        pair = jnp.concatenate([local[i][:, :steps], local[i + half][:, :steps]], axis=1)
        send_ref[:, i, :] = jnp.broadcast_to(pair, (devices, BLK))


def flows_kernel(where_ref, got_ref, travel_hbm, src_hbm, drive_ref, weight_ref, ids_ref, move_hbm,
                 flow_ref, rate_ref, travel_ref, src_ref, move_ref, padded_ref, sems, *, levels, basins):
    steps, reaches = drive_ref.shape
    count = steps.bit_length() - 1
    loads = copies(
        [(travel_hbm, travel_ref), (src_hbm, src_ref)]
        + [(move_hbm.at[k], move_ref.at[k]) for k in range(count + 1)], sems
    )
    blocks = reaches // BLK
    half = blocks // 2
    lanes = ids_ref.shape[2]
    level_id = where_ref[0]
    summed = jnp.sum(got_ref[...], axis=0)
    parts = rate_ref.shape[1] // BLK
    for k in range(2):
        for h in range(parts):
            at = 4 + k * parts + h
            rate_ref[k : k + 1, h * BLK : (h + 1) * BLK] = summed[at : at + 1]
    padded_ref[:steps, :] = jnp.zeros((steps, lanes), F32)
    rows = basins * 8
    row = iota((rows, lanes), 0)
    column = iota((rows, lanes), 1)
    inner = row % 8
    left = ((inner < half) & (column == (row // 8) * blocks + inner)).astype(BF16)
    right = ((inner < half) & (column == (row // 8) * blocks + inner + half)).astype(BF16)
    outlet = None
    chosen = jnp.zeros((steps, lanes), F32)
    for l in range(levels - 1):
        block = got_ref[l * basins : (l + 1) * basins].reshape(rows, BLK)
        block = jnp.where(iota((rows, BLK), 0) % 8 < half, block, 0.0)
        local = pick(block, left, TN)[:steps] + pick(block, right, TN)[steps:]
        if l == 0:
            outlet = local
        else:
            padded_ref[steps:, :] = outlet
            arriving = lag_sum(steps, weight_ref, l, padded_ref, True)
            member = (
                iota((lanes, lanes), 0).astype(F32) + 1.0
                == jnp.broadcast_to(ids_ref[l, 1:2, :], (lanes, lanes))
            ).astype(BF16)
            outlet = local + pick(arriving, member, NT)
        chosen = chosen + jnp.where(level_id == l + 1, outlet, 0.0)
    loads[0].wait()
    loads[1].wait()
    coef_in, coef_prev, _ = coefficients(travel_ref[...])
    source = (iota((lanes, reaches), 0) == jnp.broadcast_to(src_ref[...], (lanes, reaches))).astype(BF16)
    inflow = pick(chosen, source, NN)
    driving = coef_in * inflow + coef_prev * shift_down(inflow, 1) + drive_ref[...]
    each = range(blocks)
    loads[2].wait()
    state = [
        mm3(split2(driving[:, b * BLK : (b + 1) * BLK]), (move_ref[0, 0, b], move_ref[0, 1, b]), NN)
        for b in each
    ]
    for level in range(steps.bit_length() - 1):
        size = 1 << level
        loads[3 + level].wait()
        for b in each:
            move = (move_ref[level + 1, 0, b], move_ref[level + 1, 1, b])
            if size < 8:
                state[b] = state[b] + mm3(split2(shift_down(state[b], size)), move, NN)
            else:
                out = mm3(split2(state[b][: steps - size]), move, NN)
                state[b] = jnp.concatenate([state[b][:size], state[b][size:] + out], axis=0)
    for b in each:
        flow_ref[:, b * BLK : (b + 1) * BLK] = state[b]


def per_device(runoff, travel, downstream, inflow_src, reach_unit, rates, cotangent):
    _, steps, reaches = runoff.shape
    blocks = reaches // BLK
    levels = lax.axis_size("level")
    basins = lax.axis_size("basin")
    devices = levels * basins
    outlets = basins * blocks
    lanes = -(-outlets // BLK) * BLK
    units_here = rates.shape[1]
    halves = units_here // BLK
    count = steps.bit_length() - 1
    shape = jax.ShapeDtypeStruct
    smem = pl.BlockSpec(memory_space=pltpu.SMEM)
    vmem = pl.BlockSpec(memory_space=pltpu.VMEM)
    hbm = pl.BlockSpec(memory_space=pltpu.HBM)
    params = pltpu.CompilerParams(vmem_limit_bytes=VMEM_LIMIT)
    row_f32 = pltpu.VMEM((1, reaches), F32)
    row_i32 = pltpu.VMEM((1, reaches), jnp.int32)
    series = pltpu.VMEM((steps, reaches), F32)
    answers = pltpu.VMEM((blocks, steps, BLK), F32)
    moves_shape = (count + 1, 2, blocks, BLK, BLK)
    height = CAP + 8 * (-(-basins * CAP // BLK))
    where = jnp.stack([lax.axis_index("level"), lax.axis_index("basin")]).astype(jnp.int32)
    packet, grad, resp, moves = pl.pallas_call(
        lambda *refs: blocks_kernel(*refs, basins=basins),
        out_shape=(
            shape((devices, height, BLK), F32),
            shape((steps, reaches), F32),
            shape((blocks, steps, BLK), F32),
            shape(moves_shape, BF16),
        ),
        in_specs=[smem] + [hbm] * 5,
        out_specs=(vmem, hbm, hbm, hbm),
        scratch_shapes=[
            row_f32, row_i32, row_i32, pltpu.VMEM(rates.shape, F32), series,
            series, answers, pltpu.VMEM(moves_shape, BF16),
            pltpu.SemaphoreType.DMA((5,)), pltpu.SemaphoreType.DMA((count + 3,)),
        ],
        compiler_params=params,
        name="blocks",
    )(where, travel, downstream, inflow_src, rates, cotangent)
    got = lax.all_to_all(packet, LEVELS_AXES, 0, 0)

    def finish(got):
        sent, drive, weights, numbers, full = pl.pallas_call(
            lambda *refs: grads_kernel(*refs, levels=levels, basins=basins, units_here=units_here),
            out_shape=(
                shape((devices, 8, BLK), F32),
                shape((steps, reaches), F32),
                shape((levels, steps, lanes), F32),
                shape((levels, 8, lanes), F32),
                shape((1,), jnp.int32),
            ),
            in_specs=[smem, vmem] + [hbm] * 5,
            out_specs=(vmem,) * 4 + (smem,),
            scratch_shapes=[row_f32, row_i32, series, series, answers, series, series, series,
                            pltpu.VMEM((2 * steps, lanes), F32), pltpu.SemaphoreType.DMA((5,))],
            compiler_params=params,
            name="grads",
        )(where, got, travel, reach_unit, runoff, grad, resp)
        swapped = lax.all_to_all(sent, LEVELS_AXES, 0, 0)
        flows, totals = pl.pallas_call(
            lambda *refs: flows_kernel(*refs, levels=levels, basins=basins),
            out_shape=(shape((steps, reaches), F32), shape((2, units_here), F32)),
            in_specs=[smem, vmem, hbm, hbm, vmem, vmem, vmem, hbm],
            out_specs=(vmem,) * 2,
            scratch_shapes=[row_f32, row_i32, pltpu.VMEM(moves_shape, BF16),
                            pltpu.VMEM((2 * steps, lanes), F32), pltpu.SemaphoreType.DMA((count + 3,))],
            compiler_params=params,
            name="flows",
        )(where, swapped, travel, inflow_src, drive, weights, numbers, moves)
        return flows, totals, full[0]

    flows, totals, full = finish(got)
    flows, totals = lax.cond(
        full > CAP,
        lambda done: finish(spread_sources(got, grad, resp, travel, inflow_src))[:2],
        lambda done: done,
        (flows, totals),
    )
    return flows[None], totals


def spread_sources(got, grad, resp, travel, inflow_src):
    blocks, steps, _ = resp.shape
    basins = lax.axis_size("basin")
    basin_id = lax.axis_index("basin")
    outlets = basins * blocks
    reaches = blocks * BLK
    coef_in, coef_prev, _ = coefficients(travel)
    answer = resp.transpose(1, 0, 2).reshape(steps, reaches)
    zero = jnp.zeros((1, reaches), F32)
    back = coef_in * grad + coef_prev * jnp.concatenate([grad[1:], zero], axis=0)
    ahead = coef_in * answer + coef_prev * jnp.concatenate([zero, answer[:-1]], axis=0)
    block_of = (jnp.arange(reaches) // BLK + 1 + basin_id * blocks).astype(F32)
    table = jnp.concatenate([back, ahead, jnp.broadcast_to(block_of[None], (BLK, reaches))], axis=0)
    chosen = (inflow_src == jnp.arange(outlets)[:, None]).astype(F32)
    mine = lax.dot_general(chosen, table, NT, precision=lax.Precision.HIGHEST)
    parts = lax.all_to_all(mine.reshape(basins, blocks, 2 * steps + BLK), "basin", 0, 0).sum(axis=0)
    width = (got.shape[1] - CAP) // 8 * BLK
    place = jnp.arange(blocks) + basin_id * CAP
    onto = (jnp.arange(width)[None, :] == place[:, None]).astype(F32)
    slot_row = ((jnp.arange(blocks) + basin_id * blocks + 1).astype(F32)[:, None] * onto).sum(axis=0)
    block_row = (parts[:, 2 * steps : 2 * steps + 1] * onto).sum(axis=0)
    labels = jnp.concatenate(
        [slot_row[None], block_row[None], jnp.zeros((6, width), F32)], axis=0
    )
    labels = labels.reshape(8, width // BLK, BLK).transpose(1, 0, 2).reshape(-1, BLK)
    packet = jnp.concatenate(
        [parts[:, : 2 * steps], jnp.zeros((CAP - blocks, 2 * steps), F32), labels], axis=0
    )
    fresh = lax.all_to_all(
        jnp.broadcast_to(packet[None], got.shape), LEVELS_AXES, 0, 0
    )
    keep = jnp.arange(got.shape[1]) >= CAP + 4
    return jnp.where(keep[None, :, None], got, fresh)


def solution(mesh):
    placed = (
        P("level", None, "basin"),
        P("level", "basin"),
        P("level", "basin"),
        P("level", "basin"),
        P("level", "basin"),
        P(None, ("level", "basin")),
        P("level", None, "basin"),
    )
    return jax.shard_map(
        per_device,
        mesh=mesh,
        in_specs=placed,
        out_specs=(P("level", None, "basin"), P(None, ("level", "basin"))),
        check_vma=False,
    )
```

time: 67.2 us -> 58.2 us (0.87)
  local copies, waits for them, and re-layouts: 13.3 us -> 3.03 us
  blocking collectives: 10.5 us -> 20.6 us
  waiting for transfers between devices: 15.3 us -> 7.34 us
  starting transfers between devices: 9.23 us -> 2.77 us
  Pallas kernels: 17.5 us -> 22.6 us
  between operations: 0.67 us -> 1.4 us
    all_to_all x1, blocking collectives: 10.5 us -> 20.6 us  [per_device(): got = lax.all_to_all(packet, LEVELS_AXES, 0, 0)]
    unnamed x28 -> x18, local copies, waits for them, and re-layouts: 11.2 us -> 3.03 us
    all_to_all x2 -> x1, waiting for transfers between devices: 15.3 us -> 7.34 us  [finish(): swapped = lax.all_to_all(sent, LEVELS_AXES, 0, 0)]
    all_to_all x2 -> x1, starting transfers between devices: 9.23 us -> 2.77 us  [finish(): swapped = lax.all_to_all(sent, LEVELS_AXES, 0, 0)]
    pallas_call x3, Pallas kernels: 17.5 us -> 22.6 us  [the longest x1 10.4 us: per_device(): pl.pallas_call(lambda *refs: blocks_kernel(*refs, basins=basins), out_sha...]
    reshape x2 -> x0, local copies, waits for them, and re-layouts: 1.29 us -> none  [the longest x1 0.69 us: per_device(): rates.reshape(2 * halves, BLK)]
    broadcast_in_dim x2 -> x0, local copies, waits for them, and re-layouts: 0.72 us -> none  [the longest x1 0.72 us: per_device(): jnp.broadcast_to(packet[None], (devices, 16, BLK))]
  transfers between devices with their start and end apart: 2 -> 1, of which waited for: 2 -> 1; matrix products, arithmetic and copies ran while one was open for 1% -> 0% of each run, Pallas kernels for 0% -> 0%
where the time goes in v1:
time: 58.2 us; the launch traced here: 57.9 us
  Pallas kernels  22.6 us (39%)
  blocking collectives  20.6 us (35%)
  waiting for transfers between devices  7.34 us (13%)
  local copies, waits for them, and re-layouts  3.03 us (5%)
  starting transfers between devices  2.77 us (5%)
  between operations  1.4 us (2%)
    all_to_all x1, blocking collectives, per_device(): got = lax.all_to_all(packet, LEVELS_AXES, 0, 0)  20.6 us
    pallas_call x1, Pallas kernels, per_device(): pl.pallas_call(lambda *refs: blocks_kernel(*refs, basins=basins), out_sha...  10.4 us
    all_to_all x1, waiting for transfers between devices, finish(): swapped = lax.all_to_all(sent, LEVELS_AXES, 0, 0)  7.34 us
    pallas_call x1, Pallas kernels, finish(): pl.pallas_call(lambda *refs: grads_kernel(*refs, levels=levels, basins=ba...  7.3 us
    pallas_call x1, Pallas kernels, finish(): pl.pallas_call(lambda *refs: flows_kernel(*refs, levels=levels, basins=ba...  4.94 us
    unnamed x18, local copies, waits for them, and re-layouts  3.03 us
    all_to_all x1, starting transfers between devices, finish(): swapped = lax.all_to_all(sent, LEVELS_AXES, 0, 0)  2.77 us
  transfers between devices with their start and end apart: 1, of which 1 were waited for; matrix products, arithmetic and copies ran while one was open for 0% of the time, Pallas kernels for 0%

profile of v1, /device:TPU:0, one launch (start us, length us, event | category | flops | bytes accessed | tf_op | source)
XLA Modules:
  0.0 57.9 jit_solution(6704533977854355176)
XLA Ops:
  0.6 0.0 copy-start.4
  0.6 0.0 copy-start.5
  0.7 0.0 copy-start.6
  0.7 0.1 pad_add_fusion.refs_0_
  0.7 0.0 copy-start
  0.7 0.9 %copy-done = f32[1,64,1024]{2,1,0:T(8,128)S(1)} copy-done((f32[1,64,1024]{2,1,0:T(8,128)S(1)}, f32[1,64,1024]{2,1,0:T(8,128)}, u32[]{:S(2)}) %copy-start) | copy-done | bytes 262168
  1.7 0.0 copy-start.1
  1.7 0.7 %copy-done.1 = s32[1,1024]{1,0:T(1,128)S(1)} copy-done((s32[1,1024]{1,0:T(1,128)S(1)}, s32[1,1024]{1,0:T(1,128)}, u32[]{:S(2)}) %copy-start.1) | copy-done | bytes 4120
  2.4 0.0 copy-start.2
  2.4 0.7 %copy-done.2 = f32[2,256]{1,0:T(2,128)S(1)} copy-done((f32[2,256]{1,0:T(2,128)S(1)}, f32[2,256]{1,0:T(2,128)}, u32[]{:S(2)}) %copy-start.2) | copy-done | bytes 2072
  3.1 10.4 %blocks.1 = (f32[32,24,128]{2,1,0:T(8,128)S(1)}, f32[64,1024]{1,0:T(8,128)S(1)}, f32[8,64,128]{2,1,0:T(8,128)S(1)}, bf16[7,2,8,128,128]{4,3,2,1,0:T(8,128)(2,1)}) custom-call(s32[2]{0:T(128)S(1)} %pad_add_fusion.refs_0_, f32[1,1024]{1,0:T(1,128)} %refs_2_.5, s32[1,1024]{1,0:T(1,128)S(1)} %copy-done.1, s32[1,1024]{1,0:T(1,128)} %refs_3_.5, ...), custom_call_target="tpu_custom_call" | custom-call | tf_op jit(solution)/shard_map/blocks/pallas_call | solution.py:486
  13.5 20.6 %all_to_all.23.refs_1_ = f32[32,24,128]{2,1,0:T(8,128)S(1)} all-to-all(f32[32,24,128]{2,1,0:T(8,128)S(1)} %get-tuple-element.59), channel_id=1, replica_groups=mesh['level'=4,'basin'=8] {'level','basin'}, dimensions={0} | all-to-all | bytes 786432 | tf_op jit(solution)/shard_map/all_to_all | solution.py:504
  34.1 7.3 %grads.3 = (f32[32,8,128]{2,1,0:T(8,128)}, f32[64,1024]{1,0:T(8,128)S(1)}, f32[4,64,128]{2,1,0:T(8,128)S(1)}, f32[4,8,128]{2,1,0:T(8,128)S(1)}, s32[1]{0:T(128)}) custom-call(s32[2]{0:T(128)S(1)} %pad_add_fusion.refs_0_, f32[32,24,128]{2,1,0:T(8,128)S(1)} %all_to_all.23.refs_1_, f32[1,1024]{1,0:T(1,128)} %refs_2_.5, s32[1,1024]{1,0:T(1,128)} %refs_3_.4, ...), custom_call_target="tpu_custom_call" | custom-call | tf_op jit(solution)/shard_map/grads/pallas_call | solution.py:507
  41.4 2.8 %all-to-all-start.4 = ((f32[32,8,128]{2,1,0:T(8,128)}), f32[32,8,128]{2,1,0:T(8,128)S(1)}, u32[]{:S(2)}, u32[]{:S(2)}) async-start(f32[32,8,128]{2,1,0:T(8,128)} %get-tuple-element.63), calls=%async_computation.4 | async-start | bytes 262144 | tf_op jit(solution)/shard_map/all_to_all | solution.py:523
  44.8 7.3 %all-to-all-done.4.refs_1_ = f32[32,8,128]{2,1,0:T(8,128)S(1)} async-done(((f32[32,8,128]{2,1,0:T(8,128)}), f32[32,8,128]{2,1,0:T(8,128)S(1)}, u32[]{:S(2)}, u32[]{:S(2)}) %all-to-all-start.4) | async-done | bytes 131104 | tf_op jit(solution)/shard_map/all_to_all | solution.py:523
  52.2 4.9 %flows.3 = (f32[64,1024]{1,0:T(8,128)S(1)}, f32[2,256]{1,0:T(2,128)S(1)}) custom-call(s32[2]{0:T(128)S(1)} %pad_add_fusion.refs_0_, f32[32,8,128]{2,1,0:T(8,128)S(1)} %all-to-all-done.4.refs_1_, f32[1,1024]{1,0:T(1,128)} %refs_2_.5, s32[1,1024]{1,0:T(1,128)} %refs_3_.5, f32[64,1024]{1,0:T(8,128)S(1)} %get-tuple-element.64.refs_4_, ...), custom_call_target="tpu_custom_call" | custom-call | tf_op jit(solution)/shard_map/flows/pallas_call | solution.py:524
  57.1 0.0 copy-done.4
  57.1 0.0 copy-done.5
  57.2 0.0 copy-done.6
  57.2 0.0 copy-done.3
  57.2 0.0 copy-start.7
  57.2 0.0 copy-start.8
  57.2 0.7 %copy-done.7 = f32[1,64,1024]{2,1,0:T(8,128)} copy-done((f32[1,64,1024]{2,1,0:T(8,128)}, f32[1,64,1024]{2,1,0:T(8,128)S(1)}, u32[]{:S(2)}) %copy-start.7) | copy-done | bytes 262168
  57.9 0.0 copy-done.8
  (2 shorter events, 0.0 us)
Async XLA Ops:
  0.6 56.5 %copy-start.4 = (f32[1,1024]{1,0:T(1,128)S(1)}, f32[1,1024]{1,0:T(1,128)}, u32[]{:S(2)}) copy-start(f32[1,1024]{1,0:T(1,128)} %refs_2_.5) | copy-start | bytes 12292
  0.6 56.5 %copy-start.5 = (s32[1,1024]{1,0:T(1,128)S(1)}, s32[1,1024]{1,0:T(1,128)}, u32[]{:S(2)}) copy-start(s32[1,1024]{1,0:T(1,128)} %refs_3_.5) | copy-start | bytes 12292
  0.7 56.5 %copy-start.6 = (s32[1,1024]{1,0:T(1,128)S(1)}, s32[1,1024]{1,0:T(1,128)}, u32[]{:S(2)}) copy-start(s32[1,1024]{1,0:T(1,128)} %refs_3_.4) | copy-start | bytes 12292
  0.7 1.0 %copy-start = (f32[1,64,1024]{2,1,0:T(8,128)S(1)}, f32[1,64,1024]{2,1,0:T(8,128)}, u32[]{:S(2)}) copy-start(f32[1,64,1024]{2,1,0:T(8,128)} %refs_5_.1) | copy-start | bytes 786436
  1.7 0.7 %copy-start.1 = (s32[1,1024]{1,0:T(1,128)S(1)}, s32[1,1024]{1,0:T(1,128)}, u32[]{:S(2)}) copy-start(s32[1,1024]{1,0:T(1,128)} %refs_2_.3) | copy-start | bytes 12292
  2.4 0.7 %copy-start.2 = (f32[2,256]{1,0:T(2,128)S(1)}, f32[2,256]{1,0:T(2,128)}, u32[]{:S(2)}) copy-start(f32[2,256]{1,0:T(2,128)} %refs_4_.2) | copy-start | bytes 6148
  3.1 54.1 %copy-start.3 = (f32[1,64,1024]{2,1,0:T(8,128)S(1)}, f32[1,64,1024]{2,1,0:T(8,128)}, u32[]{:S(2)}) copy-start(f32[1,64,1024]{2,1,0:T(8,128)} %refs_4_.3) | copy-start | bytes 786436
  41.4 10.8 %all-to-all-start.4 = ((f32[32,8,128]{2,1,0:T(8,128)}), f32[32,8,128]{2,1,0:T(8,128)S(1)}, u32[]{:S(2)}, u32[]{:S(2)}) async-start(f32[32,8,128]{2,1,0:T(8,128)} %get-tuple-element.63), calls=%async_computation.4 | async-start | bytes 262144 | tf_op jit(solution)/shard_map/all_to_all | solution.py:523
  57.2 0.7 %copy-start.7 = (f32[1,64,1024]{2,1,0:T(8,128)}, f32[1,64,1024]{2,1,0:T(8,128)S(1)}, u32[]{:S(2)}) copy-start(f32[1,64,1024]{2,1,0:T(8,128)S(1)} %get-tuple-element.57) | copy-start | bytes 786436
  57.2 0.7 %copy-start.8 = (f32[2,256]{1,0:T(2,128)}, f32[2,256]{1,0:T(2,128)S(1)}, u32[]{:S(2)}) copy-start(f32[2,256]{1,0:T(2,128)S(1)} %get-tuple-element.58) | copy-start | bytes 6148

commit v2 on v1

--- a/solution.py
+++ b/solution.py
@@ -34,27 +34,52 @@
     return high, mid, (rest - mid.astype(F32)).astype(BF16)
 
 
+def beside(*parts):
+    return jnp.concatenate(parts, axis=1)
+
+
+def above(*parts):
+    return jnp.concatenate(parts, axis=0)
+
+
+def folded(product):
+    half = product.shape[1] // 2
+    return product[:, :half] + product[:, half:]
+
+
 def mm3(left, right, dims):
-    return (
-        mm(left[0], right[0], dims) + mm(left[0], right[1], dims) + mm(left[1], right[0], dims)
-    )
-
-
-def mm6(left, right, dims):
-    small = mm(left[1], right[1], dims) + mm(left[0], right[2], dims) + mm(left[2], right[0], dims)
-    return mm(left[0], right[0], dims) + (
-        mm(left[0], right[1], dims) + mm(left[1], right[0], dims) + small
-    )
+    high, low = right[0], right[1]
+    empty = jnp.zeros_like(high)
+    wide = beside(left[0], left[1])
+    if dims == NT:
+        return folded(mm(wide, above(beside(high, high), beside(low, empty)), NT))
+    return folded(mm(wide, above(beside(high, low), beside(high, empty)), NN))
+
+
+def mm6(left, right):
+    high, mid, low = right
+    first = mm(beside(left[0], left[1]), above(beside(high, mid), beside(high, mid)), NN)
+    return folded(first) + mm(beside(left[0], left[2]), above(low, high), NN)
 
 
 def pick(value, onehot, dims):
     high, mid, low = split3(value)
-    return mm(high, onehot, dims) + mm(mid, onehot, dims) + mm(low, onehot, dims)
+    if dims == TN:
+        return mm(high, onehot, TN) + mm(mid, onehot, TN) + mm(low, onehot, TN)
+    if dims == NT:
+        both = beside(onehot, onehot)
+    else:
+        both = above(onehot, onehot)
+    return mm(beside(high, mid), both, dims) + mm(low, onehot, dims)
 
 
 def pick_right(onehot, value, dims):
     high, mid, low = split3(value)
-    return mm(onehot, high, dims) + mm(onehot, mid, dims) + mm(onehot, low, dims)
+    empty = jnp.zeros_like(low)
+    wide = beside(onehot, onehot)
+    if dims == NT:
+        return folded(mm(wide, above(beside(high, mid), beside(low, empty)), NT))
+    return folded(mm(wide, above(beside(high, low), beside(mid, empty)), NN))
 
 
 def iota(shape, axis):
@@ -199,7 +224,7 @@
                 rows[b] = jnp.concatenate([rows[b], out[keep:]], axis=0)
         if level + 1 < count:
             if level < 2:
-                moves = [split3(mm6(moves[b], moves[b], NN)) for b in each]
+                moves = [split3(mm6(moves[b], moves[b])) for b in each]
             else:
                 moves = [split2(mm3(moves[b], moves[b], NN)) for b in each]
     sources = stacked(src_ref[...], blocks)
@@ -393,7 +418,7 @@
 
 
 def flows_kernel(where_ref, got_ref, travel_hbm, src_hbm, drive_ref, weight_ref, ids_ref, move_hbm,
-                 flow_ref, rate_ref, travel_ref, src_ref, move_ref, padded_ref, sems, *, levels, basins):
+                 flow_hbm, rate_ref, travel_ref, src_ref, move_ref, padded_ref, flow_ref, sems, out_sems, *, levels, basins):
     steps, reaches = drive_ref.shape
     count = steps.bit_length() - 1
     loads = copies(
@@ -456,8 +481,15 @@
             else:
                 out = mm3(split2(state[b][: steps - size]), move, NN)
                 state[b] = jnp.concatenate([state[b][:size], state[b][size:] + out], axis=0)
+    stores = []
     for b in each:
         flow_ref[:, b * BLK : (b + 1) * BLK] = state[b]
+        side = pl.ds(b * BLK, BLK)
+        copy = pltpu.make_async_copy(flow_ref.at[:, side], flow_hbm.at[0, :, side], out_sems.at[b])
+        copy.start()
+        stores.append(copy)
+    for copy in stores:
+        copy.wait()
 
 
 def per_device(runoff, travel, downstream, inflow_src, reach_unit, rates, cotangent):
@@ -482,6 +514,7 @@
     answers = pltpu.VMEM((blocks, steps, BLK), F32)
     moves_shape = (count + 1, 2, blocks, BLK, BLK)
     height = CAP + 8 * (-(-basins * CAP // BLK))
+    still = lambda *values: [pltpu.with_memory_space_constraint(value, pltpu.HBM) for value in values]
     where = jnp.stack([lax.axis_index("level"), lax.axis_index("basin")]).astype(jnp.int32)
     packet, grad, resp, moves = pl.pallas_call(
         lambda *refs: blocks_kernel(*refs, basins=basins),
@@ -500,7 +533,7 @@
         ],
         compiler_params=params,
         name="blocks",
-    )(where, travel, downstream, inflow_src, rates, cotangent)
+    )(where, *still(travel, downstream, inflow_src, rates, cotangent))
     got = lax.all_to_all(packet, LEVELS_AXES, 0, 0)
 
     def finish(got):
@@ -519,18 +552,19 @@
                             pltpu.VMEM((2 * steps, lanes), F32), pltpu.SemaphoreType.DMA((5,))],
             compiler_params=params,
             name="grads",
-        )(where, got, travel, reach_unit, runoff, grad, resp)
+        )(where, got, *still(travel, reach_unit, runoff, grad, resp))
         swapped = lax.all_to_all(sent, LEVELS_AXES, 0, 0)
         flows, totals = pl.pallas_call(
             lambda *refs: flows_kernel(*refs, levels=levels, basins=basins),
-            out_shape=(shape((steps, reaches), F32), shape((2, units_here), F32)),
+            out_shape=(shape((1, steps, reaches), F32), shape((2, units_here), F32)),
             in_specs=[smem, vmem, hbm, hbm, vmem, vmem, vmem, hbm],
-            out_specs=(vmem,) * 2,
+            out_specs=(hbm, vmem),
             scratch_shapes=[row_f32, row_i32, pltpu.VMEM(moves_shape, BF16),
-                            pltpu.VMEM((2 * steps, lanes), F32), pltpu.SemaphoreType.DMA((count + 3,))],
+                            pltpu.VMEM((2 * steps, lanes), F32), series,
+                            pltpu.SemaphoreType.DMA((count + 3,)), pltpu.SemaphoreType.DMA((blocks,))],
             compiler_params=params,
             name="flows",
-        )(where, swapped, travel, inflow_src, drive, weights, numbers, moves)
+        )(where, swapped, *still(travel, inflow_src), drive, weights, numbers, *still(moves))
         return flows, totals, full[0]
 
     flows, totals, full = finish(got)
@@ -540,7 +574,7 @@
         lambda done: done,
         (flows, totals),
     )
-    return flows[None], totals
+    return flows, totals
 
 
 def spread_sources(got, grad, resp, travel, inflow_src):

time: 58.2 us -> 53.2 us (0.914)
  local copies, waits for them, and re-layouts: 3.03 us -> 0.02 us
  Pallas kernels: 22.6 us -> 20.5 us
    unnamed x18 -> x8, local copies, waits for them, and re-layouts: 3.03 us -> 0.02 us
    pallas_call x1, Pallas kernels: 10.4 us -> 7.69 us  [per_device(): pl.pallas_call(lambda *refs: blocks_kernel(*refs, basins=basins), out_sha...]
    pallas_call x1, Pallas kernels: 4.94 us -> 5.79 us  [finish(): pl.pallas_call(lambda *refs: flows_kernel(*refs, levels=levels, basins=ba...]
where the time goes in v2:
time: 53.2 us; the launch traced here: 53 us
  blocking collectives  20.6 us (39%)
  Pallas kernels  20.5 us (39%)
  waiting for transfers between devices  7.34 us (14%)
  starting transfers between devices  2.77 us (5%)
  between operations  1.54 us (3%)
    all_to_all x1, blocking collectives, per_device(): got = lax.all_to_all(packet, LEVELS_AXES, 0, 0)  20.6 us
    pallas_call x1, Pallas kernels, per_device(): pl.pallas_call(lambda *refs: blocks_kernel(*refs, basins=basins), out_sha...  7.69 us
    all_to_all x1, waiting for transfers between devices, finish(): swapped = lax.all_to_all(sent, LEVELS_AXES, 0, 0)  7.34 us
    pallas_call x1, Pallas kernels, finish(): pl.pallas_call(lambda *refs: grads_kernel(*refs, levels=levels, basins=ba...  7.06 us
    pallas_call x1, Pallas kernels, finish(): pl.pallas_call(lambda *refs: flows_kernel(*refs, levels=levels, basins=ba...  5.79 us
    all_to_all x1, starting transfers between devices, finish(): swapped = lax.all_to_all(sent, LEVELS_AXES, 0, 0)  2.77 us
  transfers between devices with their start and end apart: 1, of which 1 were waited for; matrix products, arithmetic and copies ran while one was open for 0% of the time, Pallas kernels for 0%

profile of v2, /device:TPU:0, one launch (start us, length us, event | category | flops | bytes accessed | tf_op | source)
XLA Modules:
  0.0 53.0 jit_solution(10404138789859162572)
XLA Ops:
  0.6 0.0 copy-start.4
  0.6 0.0 copy-start.6
  0.7 0.1 pad_add_fusion.refs_0_
  0.7 7.7 %blocks.1 = (f32[32,24,128]{2,1,0:T(8,128)S(1)}, f32[64,1024]{1,0:T(8,128)}, f32[8,64,128]{2,1,0:T(8,128)}, bf16[7,2,8,128,128]{4,3,2,1,0:T(8,128)(2,1)}) custom-call(s32[2]{0:T(128)S(1)} %pad_add_fusion.refs_0_, f32[1,1024]{1,0:T(1,128)} %refs_2_.5, s32[1,1024]{1,0:T(1,128)} %refs_2_.3, s32[1,1024]{1,0:T(1,128)} %refs_3_.5, f32[2,256]{1,0:T(2,128)} %refs_4_.2, ...), custom_call_target="tpu_custom_call" | custom-call | tf_op jit(solution)/shard_map/blocks/pallas_call | solution.py:519
  8.4 0.0 copy-start
  8.4 0.0 copy-start.2
  8.5 20.6 %all_to_all.23.refs_1_ = f32[32,24,128]{2,1,0:T(8,128)S(1)} all-to-all(f32[32,24,128]{2,1,0:T(8,128)S(1)} %get-tuple-element.46), channel_id=1, replica_groups=mesh['level'=4,'basin'=8] {'level','basin'}, dimensions={0} | all-to-all | bytes 786432 | tf_op jit(solution)/shard_map/all_to_all | solution.py:537
  29.1 7.1 %grads.3 = (f32[32,8,128]{2,1,0:T(8,128)}, f32[64,1024]{1,0:T(8,128)S(1)}, f32[4,64,128]{2,1,0:T(8,128)S(1)}, f32[4,8,128]{2,1,0:T(8,128)S(1)}, s32[1]{0:T(128)}) custom-call(s32[2]{0:T(128)S(1)} %pad_add_fusion.refs_0_, f32[32,24,128]{2,1,0:T(8,128)S(1)} %all_to_all.23.refs_1_, f32[1,1024]{1,0:T(1,128)} %refs_2_.5, s32[1,1024]{1,0:T(1,128)} %refs_3_.4, ...), custom_call_target="tpu_custom_call" | custom-call | tf_op jit(solution)/shard_map/grads/pallas_call | solution.py:540
  36.2 2.8 %all-to-all-start.4 = ((f32[32,8,128]{2,1,0:T(8,128)}), f32[32,8,128]{2,1,0:T(8,128)S(1)}, u32[]{:S(2)}, u32[]{:S(2)}) async-start(f32[32,8,128]{2,1,0:T(8,128)} %get-tuple-element.50), calls=%async_computation.4 | async-start | bytes 262144 | tf_op jit(solution)/shard_map/all_to_all | solution.py:556
  39.6 7.3 %all-to-all-done.4.refs_1_ = f32[32,8,128]{2,1,0:T(8,128)S(1)} async-done(((f32[32,8,128]{2,1,0:T(8,128)}), f32[32,8,128]{2,1,0:T(8,128)S(1)}, u32[]{:S(2)}, u32[]{:S(2)}) %all-to-all-start.4) | async-done | bytes 131104 | tf_op jit(solution)/shard_map/all_to_all | solution.py:556
  46.9 5.8 %flows.3 = (f32[1,64,1024]{2,1,0:T(8,128)}, f32[2,256]{1,0:T(2,128)}) custom-call(s32[2]{0:T(128)S(1)} %pad_add_fusion.refs_0_, f32[32,8,128]{2,1,0:T(8,128)S(1)} %all-to-all-done.4.refs_1_, f32[1,1024]{1,0:T(1,128)} %refs_2_.5, s32[1,1024]{1,0:T(1,128)} %refs_3_.5, f32[64,1024]{1,0:T(8,128)S(1)} %get-tuple-element.51.refs_4_, ...), custom_call_target="tpu_custom_call" | custom-call | tf_op jit(solution)/shard_map/flows/pallas_call | solution.py:557
  52.7 0.0 copy-done.4
  52.8 0.0 copy-done.6
  52.8 0.0 copy-done
  52.8 0.0 copy-done.2
  (1 shorter events, 0.0 us)
Async XLA Ops:
  0.6 52.1 %copy-start.4 = (f32[1,1024]{1,0:T(1,128)S(1)}, f32[1,1024]{1,0:T(1,128)}, u32[]{:S(2)}) copy-start(f32[1,1024]{1,0:T(1,128)} %refs_2_.5) | copy-start | bytes 12292
  0.6 52.1 %copy-start.6 = (s32[1,1024]{1,0:T(1,128)S(1)}, s32[1,1024]{1,0:T(1,128)}, u32[]{:S(2)}) copy-start(s32[1,1024]{1,0:T(1,128)} %refs_3_.5) | copy-start | bytes 12292
  8.4 44.3 %copy-start = (f32[64,1024]{1,0:T(8,128)S(1)}, f32[64,1024]{1,0:T(8,128)}, u32[]{:S(2)}) copy-start(f32[64,1024]{1,0:T(8,128)} %get-tuple-element.47.refs_5_) | copy-start | bytes 786436
  8.4 44.3 %copy-start.2 = (f32[8,64,128]{2,1,0:T(8,128)S(1)}, f32[8,64,128]{2,1,0:T(8,128)}, u32[]{:S(2)}) copy-start(f32[8,64,128]{2,1,0:T(8,128)} %get-tuple-element.48.refs_6_) | copy-start | bytes 786436
  36.2 10.8 %all-to-all-start.4 = ((f32[32,8,128]{2,1,0:T(8,128)}), f32[32,8,128]{2,1,0:T(8,128)S(1)}, u32[]{:S(2)}, u32[]{:S(2)}) async-start(f32[32,8,128]{2,1,0:T(8,128)} %get-tuple-element.50), calls=%async_computation.4 | async-start | bytes 262144 | tf_op jit(solution)/shard_map/all_to_all | solution.py:556

commit v3 on v2

--- a/solution.py
+++ b/solution.py
@@ -16,6 +16,7 @@
 TN = (((0,), (0,)), ((), ()))
 VMEM_LIMIT = 48 << 20
 CAP = 16
+NEAR = 5
 
 
 def mm(left, right, dims):
@@ -124,6 +125,16 @@
 
 def stacked(row, blocks):
     return jnp.concatenate([row[:, b * BLK : (b + 1) * BLK] for b in range(blocks)], axis=0)
+
+
+def still(*values):
+    return [pltpu.with_memory_space_constraint(value, pltpu.HBM) for value in values]
+
+
+def relay_kernel(*refs):
+    half = len(refs) // 2
+    for copy in copies(list(zip(refs[:half], refs[half:-1])), refs[-1]):
+        copy.wait()
 
 
 def blocks_kernel(where_ref, travel_hbm, down_hbm, src_hbm, rates_hbm, cot_hbm,
@@ -282,38 +293,42 @@
         copy.wait()
 
 
-def lag_sum(out_rows, weight_ref, level, padded_ref, forward):
-    steps = out_rows
-    total = jnp.zeros((steps, padded_ref.shape[1]), F32)
+def lag_sum(steps, weight_ref, level, padded_ref, forward):
+    tiles = steps // 8
+    total = [jnp.zeros((8, padded_ref.shape[1]), F32)] * tiles
     for lag in range(steps):
-        start = steps - lag if forward else lag
-        total = total + weight_ref[level, lag : lag + 1, :] * padded_ref[start : start + steps, :]
-    return total
-
-
-def lookup_rows(unit, units_here, halves, width):
-    lane = BLK
-    owner = unit // units_here
-    inside = unit - owner * units_here
-    half = inside // lane
-    low = inside - half * lane
-    row = 8 * owner + 4 + half
-    return row, row + halves, low
+        weight = weight_ref[level, lag : lag + 1, :]
+        if forward:
+            first, last = lag // 8, tiles
+            start = steps - lag + 8 * first
+        else:
+            first, last = 0, tiles - lag // 8
+            start = lag
+        shifted = padded_ref[start : start + 8 * (last - first), :]
+        for at in range(first, last):
+            total[at] = total[at] + weight * shifted[8 * (at - first) : 8 * (at - first) + 8]
+    return jnp.concatenate(total, axis=0)
 
 
 def grads_kernel(where_ref, got_ref, travel_hbm, unit_hbm, rain_hbm, grad_hbm, resp_hbm,
-                 send_ref, drive_ref, weight_ref, ids_ref, full_ref,
+                 send_ref, drive_ref, weight_ref, ids_ref,
                  travel_ref, unit_ref, rain_ref, grad_ref, resp_ref,
                  lateral_ref, fast_ref, slow_ref, padded_ref, sems, *, levels, basins, units_here):
-    steps, reaches = rain_ref.shape
+    steps, reaches = grad_ref.shape
+    blocks = reaches // BLK
+    pitch = steps + 8
+    rains = [
+        (rain_hbm.at[0, :, pl.ds(b * BLK, BLK)], rain_ref.at[pl.ds(b * pitch, steps)])
+        for b in range(blocks)
+    ]
     loads = copies(
-        [(travel_hbm, travel_ref), (unit_hbm, unit_ref), (rain_hbm.at[0], rain_ref),
-         (resp_hbm, resp_ref), (grad_hbm, grad_ref)], sems
+        [(travel_hbm, travel_ref), (unit_hbm, unit_ref)] + rains
+        + [(resp_hbm, resp_ref), (grad_hbm, grad_ref)], sems
     )
-    blocks = reaches // BLK
     devices = levels * basins
     lanes = ids_ref.shape[2]
-    full_ref[0] = jnp.max(got_ref[basins:, CAP + 2 : CAP + 3, :]).astype(jnp.int32)
+    most = jnp.max(got_ref[basins:, CAP : CAP + 8, :], axis=0)[2:3, :]
+    ids_ref[0] = jnp.broadcast_to(jnp.max(most, axis=1, keepdims=True), (8, lanes))
     outlets = basins * blocks
     halves = units_here // BLK
     level_id = where_ref[0]
@@ -356,43 +371,55 @@
     loads[0].wait()
     loads[1].wait()
     _, _, coef_keep = coefficients(travel_ref[...])
-    fast_row, slow_row, low = lookup_rows(unit_ref[...], units_here, halves, reaches)
+    unit_row = unit_ref[...] // BLK
+    low = unit_ref[...] - unit_row * BLK
     places = (iota((BLK, reaches), 0) == jnp.broadcast_to(low, (BLK, reaches))).astype(BF16)
+    owned = devices * halves
+    at = iota((2 * owned, devices * 8), 0)
+    kind = at // owned
+    inside = at - kind * owned
+    line = inside // halves * 8 + 4 + kind * halves + inside % halves
+    compact = (iota((2 * owned, devices * 8), 1) == line).astype(BF16)
     table = got_ref[:, CAP : CAP + 8, :].reshape(devices * 8, BLK)
-    spread = pick(table, places, NN)
-    row_of = iota((devices * 8, reaches), 0)
-    fast_at = row_of == fast_row
-    slow_at = row_of == slow_row
-    fast_rate = jnp.sum(jnp.where(fast_at, spread, 0.0), axis=0, keepdims=True)
-    slow_rate = jnp.sum(jnp.where(slow_at, spread, 0.0), axis=0, keepdims=True)
+    spread = pick(pick_right(compact, table, NN), places, NN)
+    row_at = iota((owned, reaches), 0) == jnp.broadcast_to(unit_row, (owned, reaches))
+    fast_rate = jnp.sum(jnp.where(row_at, spread[:owned], 0.0), axis=0, keepdims=True)
+    slow_rate = jnp.sum(jnp.where(row_at, spread[owned:], 0.0), axis=0, keepdims=True)
     fast_keep = jnp.exp(-fast_rate)
     slow_keep = jnp.exp(-slow_rate)
-    fast_in = (1.0 - fast_keep) * SPLIT_FAST
-    slow_in = (1.0 - slow_keep) * (1.0 - SPLIT_FAST)
-    loads[2].wait()
-    zero = jnp.zeros((1, reaches), F32)
+    for copy in loads[2 : 2 + blocks]:
+        copy.wait()
+    fast_by = stacked(fast_keep, blocks)
+    slow_by = stacked(slow_keep, blocks)
+    fast_gain = (1.0 - fast_by) * SPLIT_FAST
+    slow_gain = (1.0 - slow_by) * (1.0 - SPLIT_FAST)
+    zero = jnp.zeros((blocks, BLK), F32)
     fast, slow, fast_sens, slow_sens = zero, zero, zero, zero
     for step in range(steps):
-        rain = rain_ref[step : step + 1, :]
-        fast_sens = fast_keep * fast_sens + (fast - SPLIT_FAST * rain)
-        slow_sens = slow_keep * slow_sens + (slow - (1.0 - SPLIT_FAST) * rain)
-        fast = fast_keep * fast + fast_in * rain
-        slow = slow_keep * slow + slow_in * rain
-        lateral_ref[step : step + 1, :] = fast + slow
-        fast_ref[step : step + 1, :] = fast_sens
-        slow_ref[step : step + 1, :] = slow_sens
-    drive = (1.0 - coef_keep) * lateral_ref[...]
-    drive_ref[...] = drive
-    loads[3].wait()
+        at = pl.ds(step, blocks, stride=pitch)
+        rain = rain_ref[at, :]
+        fast_sens = fast_by * fast_sens + (fast - SPLIT_FAST * rain)
+        slow_sens = slow_by * slow_sens + (slow - (1.0 - SPLIT_FAST) * rain)
+        fast = fast_by * fast + fast_gain * rain
+        slow = slow_by * slow + slow_gain * rain
+        lateral_ref[at, :] = fast + slow
+        fast_ref[at, :] = fast_sens
+        slow_ref[at, :] = slow_sens
+    scale = 1.0 - coef_keep
+    drives = []
+    for b in range(blocks):
+        drives.append(scale[:, b * BLK : (b + 1) * BLK] * lateral_ref[b * pitch : b * pitch + steps, :])
+        drive_ref[b] = drives[b]
+    loads[2 + blocks].wait()
     local = []
     for b in range(blocks):
         padded = jnp.concatenate(
-            [drive[:, b * BLK : (b + 1) * BLK], jnp.zeros((BLK - steps, BLK), F32)], axis=0
+            [drives[b], jnp.zeros((BLK - steps, BLK), F32)], axis=0
         )
         product = mm3(split2(resp_ref[b]), split2(padded), NT)
         skewed = pltpu.roll(product, 0, 1, stride=1, stride_axis=0)
         local.append(jnp.sum(skewed, axis=0, keepdims=True))
-    loads[4].wait()
+    loads[3 + blocks].wait()
     fast_sum = []
     slow_sum = []
     for b in range(blocks):
@@ -403,29 +430,59 @@
             spreadout = jnp.where((at & (1 << bit)) != 0, moved, spreadout)
         resp = jnp.concatenate([resp_ref[b], jnp.zeros((BLK - steps, BLK), F32)], axis=0)
         grad = grad_ref[:, b * BLK : (b + 1) * BLK] + mm3(split2(spreadout), split2(resp), NN)
-        side = slice(b * BLK, (b + 1) * BLK)
-        fast_sum.append(jnp.sum(grad * fast_ref[:, side], axis=0, keepdims=True))
-        slow_sum.append(jnp.sum(grad * slow_ref[:, side], axis=0, keepdims=True))
-    scale = 1.0 - coef_keep
+        side = slice(b * pitch, b * pitch + steps)
+        fast_sum.append(jnp.sum(grad * fast_ref[side, :], axis=0, keepdims=True))
+        slow_sum.append(jnp.sum(grad * slow_ref[side, :], axis=0, keepdims=True))
     fast_grad = -fast_keep * scale * jnp.concatenate(fast_sum, axis=1)
     slow_grad = -slow_keep * scale * jnp.concatenate(slow_sum, axis=1)
-    terms = jnp.where(fast_at, fast_grad, 0.0) + jnp.where(slow_at, slow_grad, 0.0)
-    send_ref[...] = pick(terms, places, NT).reshape(devices, 8, BLK)
+    terms = [
+        jnp.where(row_at, jnp.broadcast_to(piece.astype(F32), (owned, reaches)), 0.0).astype(BF16)
+        for pieces in zip(split3(fast_grad), split3(slow_grad))
+        for piece in pieces
+    ]
+    parts = mm(jnp.concatenate(terms, axis=0), places, NT)
+    summed = parts[: 2 * owned] + parts[2 * owned : 4 * owned] + parts[4 * owned :]
+    at = iota((devices * 8, 2 * owned), 1)
+    kind = at // owned
+    inside = at - kind * owned
+    line = inside // halves * 8 + 4 + kind * halves + inside % halves
+    expand = (iota((devices * 8, 2 * owned), 0) == line).astype(BF16)
+    send_ref[...] = pick_right(expand, summed, NN).reshape(devices, 8, BLK)
     half = blocks // 2
     for i in range(half):
         pair = jnp.concatenate([local[i][:, :steps], local[i + half][:, :steps]], axis=1)
         send_ref[:, i, :] = jnp.broadcast_to(pair, (devices, BLK))
 
 
-def flows_kernel(where_ref, got_ref, travel_hbm, src_hbm, drive_ref, weight_ref, ids_ref, move_hbm,
-                 flow_hbm, rate_ref, travel_ref, src_ref, move_ref, padded_ref, flow_ref, sems, out_sems, *, levels, basins):
-    steps, reaches = drive_ref.shape
-    count = steps.bit_length() - 1
+def fetch_kernel(ids_ref, travel_hbm, src_hbm, move_hbm, *refs):
+    move_refs = refs[:NEAR]
+    coef_ref, source_ref, full_ref, travel_ref, src_ref, sems = refs[NEAR:]
     loads = copies(
         [(travel_hbm, travel_ref), (src_hbm, src_ref)]
-        + [(move_hbm.at[k], move_ref.at[k]) for k in range(count + 1)], sems
+        + [(move_hbm.at[k], move_refs[k]) for k in range(NEAR)], sems
     )
-    blocks = reaches // BLK
+    full_ref[0] = jnp.max(ids_ref[0, 0:1, :]).astype(jnp.int32)
+    loads[0].wait()
+    loads[1].wait()
+    coef_in, coef_prev, _ = coefficients(travel_ref[...])
+    coef_ref[0:1, :] = coef_in
+    coef_ref[1:2, :] = coef_prev
+    lanes, reaches = source_ref.shape
+    held = iota((lanes, reaches), 0) == jnp.broadcast_to(src_ref[...], (lanes, reaches))
+    source_ref[...] = held.astype(BF16)
+    for copy in loads[2:]:
+        copy.wait()
+
+
+def flows_kernel(where_ref, got_ref, coef_ref, source_ref, drive_ref, weight_ref, ids_ref, *refs,
+                 levels, basins):
+    near_refs = refs[:NEAR]
+    move_hbm, flow_hbm, rate_hbm, far_ref, padded_ref, flow_ref, rate_ref, in_sems, out_sems = refs[NEAR:]
+    blocks, steps, _ = drive_ref.shape
+    far = move_hbm.shape[0] - NEAR
+    loads = copies([(move_hbm.at[NEAR + k], far_ref.at[k]) for k in range(far)], in_sems)
+    move_refs = [*near_refs] + [far_ref.at[k] for k in range(far)]
+    reaches = blocks * BLK
     half = blocks // 2
     lanes = ids_ref.shape[2]
     level_id = where_ref[0]
@@ -435,6 +492,8 @@
         for h in range(parts):
             at = 4 + k * parts + h
             rate_ref[k : k + 1, h * BLK : (h + 1) * BLK] = summed[at : at + 1]
+    stores = [pltpu.make_async_copy(rate_ref, rate_hbm, out_sems.at[blocks])]
+    stores[0].start()
     padded_ref[:steps, :] = jnp.zeros((steps, lanes), F32)
     rows = basins * 8
     row = iota((rows, lanes), 0)
@@ -459,29 +518,24 @@
             ).astype(BF16)
             outlet = local + pick(arriving, member, NT)
         chosen = chosen + jnp.where(level_id == l + 1, outlet, 0.0)
-    loads[0].wait()
-    loads[1].wait()
-    coef_in, coef_prev, _ = coefficients(travel_ref[...])
-    source = (iota((lanes, reaches), 0) == jnp.broadcast_to(src_ref[...], (lanes, reaches))).astype(BF16)
-    inflow = pick(chosen, source, NN)
-    driving = coef_in * inflow + coef_prev * shift_down(inflow, 1) + drive_ref[...]
+    inflow = pick(chosen, source_ref[...], NN)
+    driving = coef_ref[0:1, :] * inflow + coef_ref[1:2, :] * shift_down(inflow, 1)
     each = range(blocks)
-    loads[2].wait()
     state = [
-        mm3(split2(driving[:, b * BLK : (b + 1) * BLK]), (move_ref[0, 0, b], move_ref[0, 1, b]), NN)
+        mm3(split2(driving[:, b * BLK : (b + 1) * BLK] + drive_ref[b]), (move_refs[0][0, b], move_refs[0][1, b]), NN)
         for b in each
     ]
     for level in range(steps.bit_length() - 1):
         size = 1 << level
-        loads[3 + level].wait()
         for b in each:
-            move = (move_ref[level + 1, 0, b], move_ref[level + 1, 1, b])
+            if b == 0 and level + 1 >= NEAR:
+                loads[level + 1 - NEAR].wait()
+            move = (move_refs[level + 1][0, b], move_refs[level + 1][1, b])
             if size < 8:
                 state[b] = state[b] + mm3(split2(shift_down(state[b], size)), move, NN)
             else:
                 out = mm3(split2(state[b][: steps - size]), move, NN)
                 state[b] = jnp.concatenate([state[b][:size], state[b][size:] + out], axis=0)
-    stores = []
     for b in each:
         flow_ref[:, b * BLK : (b + 1) * BLK] = state[b]
         side = pl.ds(b * BLK, BLK)
@@ -511,10 +565,10 @@
     row_f32 = pltpu.VMEM((1, reaches), F32)
     row_i32 = pltpu.VMEM((1, reaches), jnp.int32)
     series = pltpu.VMEM((steps, reaches), F32)
+    stack = pltpu.VMEM((blocks * (steps + 8), BLK), F32)
     answers = pltpu.VMEM((blocks, steps, BLK), F32)
     moves_shape = (count + 1, 2, blocks, BLK, BLK)
     height = CAP + 8 * (-(-basins * CAP // BLK))
-    still = lambda *values: [pltpu.with_memory_space_constraint(value, pltpu.HBM) for value in values]
     where = jnp.stack([lax.axis_index("level"), lax.axis_index("basin")]).astype(jnp.int32)
     packet, grad, resp, moves = pl.pallas_call(
         lambda *refs: blocks_kernel(*refs, basins=basins),
@@ -537,47 +591,72 @@
     got = lax.all_to_all(packet, LEVELS_AXES, 0, 0)
 
     def finish(got):
-        sent, drive, weights, numbers, full = pl.pallas_call(
+        sent, drive, weights, numbers = pl.pallas_call(
             lambda *refs: grads_kernel(*refs, levels=levels, basins=basins, units_here=units_here),
             out_shape=(
                 shape((devices, 8, BLK), F32),
-                shape((steps, reaches), F32),
+                shape((blocks, steps, BLK), F32),
                 shape((levels, steps, lanes), F32),
                 shape((levels, 8, lanes), F32),
-                shape((1,), jnp.int32),
             ),
             in_specs=[smem, vmem] + [hbm] * 5,
-            out_specs=(vmem,) * 4 + (smem,),
-            scratch_shapes=[row_f32, row_i32, series, series, answers, series, series, series,
-                            pltpu.VMEM((2 * steps, lanes), F32), pltpu.SemaphoreType.DMA((5,))],
+            out_specs=(vmem,) * 4,
+            scratch_shapes=[row_f32, row_i32, stack, series, answers, stack, stack, stack,
+                            pltpu.VMEM((2 * steps, lanes), F32), pltpu.SemaphoreType.DMA((blocks + 4,))],
             compiler_params=params,
             name="grads",
         )(where, got, *still(travel, reach_unit, runoff, grad, resp))
         swapped = lax.all_to_all(sent, LEVELS_AXES, 0, 0)
+        *near_moves, coefs, source, full = pl.pallas_call(
+            fetch_kernel,
+            out_shape=(
+                *[shape(moves_shape[1:], BF16)] * NEAR,
+                shape((2, reaches), F32),
+                shape((lanes, reaches), BF16),
+                shape((1,), jnp.int32),
+            ),
+            in_specs=[vmem] + [hbm] * 3,
+            out_specs=(vmem,) * (NEAR + 2) + (smem,),
+            scratch_shapes=[row_f32, row_i32, pltpu.SemaphoreType.DMA((NEAR + 2,))],
+            compiler_params=params,
+            name="fetch",
+        )(numbers, *still(travel, inflow_src, moves))
+        near = lambda *values: [pltpu.with_memory_space_constraint(value, pltpu.VMEM) for value in values]
         flows, totals = pl.pallas_call(
             lambda *refs: flows_kernel(*refs, levels=levels, basins=basins),
             out_shape=(shape((1, steps, reaches), F32), shape((2, units_here), F32)),
-            in_specs=[smem, vmem, hbm, hbm, vmem, vmem, vmem, hbm],
-            out_specs=(hbm, vmem),
-            scratch_shapes=[row_f32, row_i32, pltpu.VMEM(moves_shape, BF16),
+            in_specs=[smem] + [vmem] * (6 + NEAR) + [hbm],
+            out_specs=(hbm, hbm),
+            scratch_shapes=[pltpu.VMEM((count + 1 - NEAR, *moves_shape[1:]), BF16),
                             pltpu.VMEM((2 * steps, lanes), F32), series,
-                            pltpu.SemaphoreType.DMA((count + 3,)), pltpu.SemaphoreType.DMA((blocks,))],
+                            pltpu.VMEM((2, units_here), F32),
+                            pltpu.SemaphoreType.DMA((count + 1 - NEAR,)),
+                            pltpu.SemaphoreType.DMA((blocks + 1,))],
             compiler_params=params,
             name="flows",
-        )(where, swapped, *still(travel, inflow_src), drive, weights, numbers, *still(moves))
+        )(where, swapped, *near(coefs, source), drive, weights, numbers, *near(*near_moves), *still(moves))
         return flows, totals, full[0]
 
     flows, totals, full = finish(got)
     flows, totals = lax.cond(
         full > CAP,
-        lambda done: finish(spread_sources(got, grad, resp, travel, inflow_src))[:2],
+        lambda done: finish(spread_sources(got.shape, grad, resp, travel, inflow_src, rates))[:2],
         lambda done: done,
         (flows, totals),
     )
     return flows, totals
 
 
-def spread_sources(got, grad, resp, travel, inflow_src):
+def spread_sources(packet_shape, grad, resp, travel, inflow_src, rates):
+    values = (grad, resp, travel, inflow_src, rates)
+    grad, resp, travel, inflow_src, rates = pl.pallas_call(
+        relay_kernel,
+        out_shape=tuple(jax.ShapeDtypeStruct(value.shape, value.dtype) for value in values),
+        in_specs=[pl.BlockSpec(memory_space=pltpu.HBM)] * len(values),
+        out_specs=(pl.BlockSpec(memory_space=pltpu.HBM),) * len(values),
+        scratch_shapes=[pltpu.SemaphoreType.DMA((len(values),))],
+        name="relay",
+    )(*still(*values))
     blocks, steps, _ = resp.shape
     basins = lax.axis_size("basin")
     basin_id = lax.axis_index("basin")
@@ -593,7 +672,7 @@
     chosen = (inflow_src == jnp.arange(outlets)[:, None]).astype(F32)
     mine = lax.dot_general(chosen, table, NT, precision=lax.Precision.HIGHEST)
     parts = lax.all_to_all(mine.reshape(basins, blocks, 2 * steps + BLK), "basin", 0, 0).sum(axis=0)
-    width = (got.shape[1] - CAP) // 8 * BLK
+    width = (packet_shape[1] - CAP) // 8 * BLK
     place = jnp.arange(blocks) + basin_id * CAP
     onto = (jnp.arange(width)[None, :] == place[:, None]).astype(F32)
     slot_row = ((jnp.arange(blocks) + basin_id * blocks + 1).astype(F32)[:, None] * onto).sum(axis=0)
@@ -601,15 +680,13 @@
     labels = jnp.concatenate(
         [slot_row[None], block_row[None], jnp.zeros((6, width), F32)], axis=0
     )
+    rate_rows = rates.reshape(-1, BLK)
+    labels = labels.at[4 : 4 + rate_rows.shape[0], :BLK].set(rate_rows)
     labels = labels.reshape(8, width // BLK, BLK).transpose(1, 0, 2).reshape(-1, BLK)
     packet = jnp.concatenate(
         [parts[:, : 2 * steps], jnp.zeros((CAP - blocks, 2 * steps), F32), labels], axis=0
     )
-    fresh = lax.all_to_all(
-        jnp.broadcast_to(packet[None], got.shape), LEVELS_AXES, 0, 0
-    )
-    keep = jnp.arange(got.shape[1]) >= CAP + 4
-    return jnp.where(keep[None, :, None], got, fresh)
+    return lax.all_to_all(jnp.broadcast_to(packet[None], packet_shape), LEVELS_AXES, 0, 0)
 
 
 def solution(mesh):

time: 53.2 us -> 50.1 us (0.942)
  waiting for transfers between devices: 7.34 us -> 5.23 us
  Pallas kernels: 20.5 us -> 19.5 us
    pallas_call x0 -> x1, Pallas kernels: none -> 2.29 us  [finish(): pl.pallas_call(fetch_kernel, out_shape=(*[shape(moves_shape[1:], BF16)] *...]
    all_to_all x1, waiting for transfers between devices: 7.34 us -> 5.23 us  [finish(): swapped = lax.all_to_all(sent, LEVELS_AXES, 0, 0)]
    pallas_call x1, Pallas kernels: 7.06 us -> 5.39 us  [finish(): pl.pallas_call(lambda *refs: grads_kernel(*refs, levels=levels, basins=ba...]
    pallas_call x1, Pallas kernels: 5.79 us -> 4.15 us  [finish(): pl.pallas_call(lambda *refs: flows_kernel(*refs, levels=levels, basins=ba...]
  transfers between devices with their start and end apart: 1 -> 1, of which waited for: 1 -> 1; matrix products, arithmetic and copies ran while one was open for 0% -> 0% of each run, Pallas kernels for 0% -> 5%
where the time goes in v3:
time: 50.1 us; the launch traced here: 49.8 us
  blocking collectives  20.6 us (41%)
  Pallas kernels  19.5 us (39%)
  waiting for transfers between devices  5.23 us (10%)
  starting transfers between devices  2.59 us (5%)
  between operations  1.5 us (3%)
    all_to_all x1, blocking collectives, per_device(): got = lax.all_to_all(packet, LEVELS_AXES, 0, 0)  20.6 us
    pallas_call x1, Pallas kernels, per_device(): pl.pallas_call(lambda *refs: blocks_kernel(*refs, basins=basins), out_sha...  7.68 us
    pallas_call x1, Pallas kernels, finish(): pl.pallas_call(lambda *refs: grads_kernel(*refs, levels=levels, basins=ba...  5.39 us
    all_to_all x1, waiting for transfers between devices, finish(): swapped = lax.all_to_all(sent, LEVELS_AXES, 0, 0)  5.23 us
    pallas_call x1, Pallas kernels, finish(): pl.pallas_call(lambda *refs: flows_kernel(*refs, levels=levels, basins=ba...  4.15 us
    all_to_all x1, starting transfers between devices, finish(): swapped = lax.all_to_all(sent, LEVELS_AXES, 0, 0)  2.59 us
    pallas_call x1, Pallas kernels, finish(): pl.pallas_call(fetch_kernel, out_shape=(*[shape(moves_shape[1:], BF16)] *...  2.29 us
  transfers between devices with their start and end apart: 1, of which 1 were waited for; matrix products, arithmetic and copies ran while one was open for 0% of the time, Pallas kernels for 5%

profile of v3, /device:TPU:0, one launch (start us, length us, event | category | flops | bytes accessed | tf_op | source)
XLA Modules:
  0.0 49.8 jit_solution(5044178922613179126)
XLA Ops:
  0.6 0.1 pad_add_fusion.refs_0_
  0.7 7.7 %blocks.1 = (f32[32,24,128]{2,1,0:T(8,128)S(1)}, f32[64,1024]{1,0:T(8,128)}, f32[8,64,128]{2,1,0:T(8,128)}, bf16[7,2,8,128,128]{4,3,2,1,0:T(8,128)(2,1)}) custom-call(s32[2]{0:T(128)S(1)} %pad_add_fusion.refs_0_, f32[1,1024]{1,0:T(1,128)} %travel_hbm.1, s32[1,1024]{1,0:T(1,128)} %refs_2_.2, s32[1,1024]{1,0:T(1,128)} %src_hbm.1, f32[2,256]{1,0:T(2,128)} %refs_4_.2, ...), custom_call_target="tpu_custom_call" | custom-call | tf_op jit(solution)/shard_map/blocks/pallas_call | solution.py:573
  8.4 20.6 %all_to_all.23.refs_1_ = f32[32,24,128]{2,1,0:T(8,128)S(1)} all-to-all(f32[32,24,128]{2,1,0:T(8,128)S(1)} %get-tuple-element.77), channel_id=1, replica_groups=mesh['level'=4,'basin'=8] {'level','basin'}, dimensions={0} | all-to-all | bytes 786432 | tf_op jit(solution)/shard_map/all_to_all | solution.py:591
  29.0 5.4 %grads.3 = (f32[32,8,128]{2,1,0:T(8,128)}, f32[8,64,128]{2,1,0:T(8,128)S(1)}, f32[4,64,128]{2,1,0:T(8,128)S(1)}, f32[4,8,128]{2,1,0:T(8,128)S(1)}) custom-call(s32[2]{0:T(128)S(1)} %pad_add_fusion.refs_0_, f32[32,24,128]{2,1,0:T(8,128)S(1)} %all_to_all.23.refs_1_, f32[1,1024]{1,0:T(1,128)} %travel_hbm.1, s32[1,1024]{1,0:T(1,128)} %refs_3_.3, ...), custom_call_target="tpu_custom_call" | custom-call | tf_op jit(solution)/shard_map/grads/pallas_call | solution.py:594
  34.4 2.6 %all-to-all-start.4 = ((f32[32,8,128]{2,1,0:T(8,128)}), f32[32,8,128]{2,1,0:T(8,128)S(1)}, u32[]{:S(2)}, u32[]{:S(2)}) async-start(f32[32,8,128]{2,1,0:T(8,128)} %get-tuple-element.83), calls=%async_computation.4 | async-start | bytes 262144 | tf_op jit(solution)/shard_map/all_to_all | solution.py:609
  37.0 2.3 %fetch.3 = (bf16[2,8,128,128]{3,2,1,0:T(8,128)(2,1)S(1)}, bf16[2,8,128,128]{3,2,1,0:T(8,128)(2,1)S(1)}, bf16[2,8,128,128]{3,2,1,0:T(8,128)(2,1)S(1)}, bf16[2,8,1...) custom-call(f32[4,8,128]{2,1,0:T(8,128)S(1)} %get-tuple-element.80.i, ...), custom_call_target="tpu_custom_call" | custom-call | tf_op jit(solution)/shard_map/fetch/pallas_call | solution.py:610
  40.0 5.2 %all-to-all-done.4.refs_1_ = f32[32,8,128]{2,1,0:T(8,128)S(1)} async-done(((f32[32,8,128]{2,1,0:T(8,128)}), f32[32,8,128]{2,1,0:T(8,128)S(1)}, u32[]{:S(2)}, u32[]{:S(2)}) %all-to-all-start.4) | async-done | bytes 131104 | tf_op jit(solution)/shard_map/all_to_all | solution.py:609
  45.2 4.2 %flows.3 = (f32[1,64,1024]{2,1,0:T(8,128)}, f32[2,256]{1,0:T(2,128)}) custom-call(s32[2]{0:T(128)S(1)} %pad_add_fusion.refs_0_, f32[32,8,128]{2,1,0:T(8,128)S(1)} %all-to-all-done.4.refs_1_, f32[2,1024]{1,0:T(2,128)S(1)} %get-tuple-element.84.refs_2_, bf16[128,1024]{1,0:T(8,128)(2,1)S(1)} %get-tuple-element.85.refs_3_, ...), custom_call_target="tpu_custom_call" | custom-call | tf_op jit(solution)/shard_map/flows/pallas_call | solution.py:625
  49.4 0.2 conditional.1
Async XLA Ops:
  34.4 10.8 %all-to-all-start.4 = ((f32[32,8,128]{2,1,0:T(8,128)}), f32[32,8,128]{2,1,0:T(8,128)S(1)}, u32[]{:S(2)}, u32[]{:S(2)}) async-start(f32[32,8,128]{2,1,0:T(8,128)} %get-tuple-element.83), calls=%async_computation.4 | async-start | bytes 262144 | tf_op jit(solution)/shard_map/all_to_all | solution.py:609

commit v4 on v3

--- a/solution.py
+++ b/solution.py
@@ -8,7 +8,8 @@
 BLK = 128
 SPLIT_FAST = 0.6
 MUSK_X = 0.2
-LEVELS_AXES = ("level", "basin")
+BASIN_AXES = ("column", "core")
+LEVELS_AXES = ("level", "column", "core")
 F32 = jnp.float32
 BF16 = jnp.bfloat16
 NN = (((1,), (0,)), ((), ()))
@@ -131,6 +132,11 @@
     return [pltpu.with_memory_space_constraint(value, pltpu.HBM) for value in values]
 
 
+def label_lane(basin_id, basins):
+    column = basin_id // 2
+    return ((basin_id - 2 * column) * (basins // 2) + column) * CAP
+
+
 def relay_kernel(*refs):
     half = len(refs) // 2
     for copy in copies(list(zip(refs[:half], refs[half:-1])), refs[-1]):
@@ -143,7 +149,7 @@
                   grad_ref, resp_ref, move_ref, in_sems, out_sems, *, basins):
     steps, reaches = cot_ref.shape
     blocks = reaches // BLK
-    devices, height, _ = packet_ref.shape
+    copies_out, height, _ = packet_ref.shape
     width = (height - CAP) // 8 * BLK
     each = range(blocks)
     loads = copies(
@@ -243,6 +249,7 @@
     upper = (iota((BLK, BLK), 0) <= iota((BLK, BLK), 1)).astype(BF16)
     ranks = mm(held.astype(BF16), upper, NN)
     basin_id = where_ref[1]
+    first_lane = label_lane(basin_id, basins)
     offset = jnp.zeros((1, 1), F32)
     packed = jnp.zeros((CAP, 2 * steps), F32)
     labels = jnp.zeros((8, width), F32)
@@ -268,7 +275,7 @@
             axis=0,
         )
         packed = packed + pick_right(chosen, sent, NT)
-        lane_at = iota((width, BLK), 0) - basin_id * CAP
+        lane_at = iota((width, BLK), 0) - first_lane
         wide = (
             (jnp.broadcast_to(rank, (width, BLK)) == lane_at.astype(F32) + 1.0) & (lane_at < CAP)
         ).astype(BF16)
@@ -287,8 +294,8 @@
         else:
             tail = [jnp.zeros((4, BLK), F32)]
         piece = jnp.concatenate([rows_here] + tail, axis=0)
-        packet_ref[:, first : first + 8, :] = jnp.broadcast_to(piece[None], (devices, 8, BLK))
-    packet_ref[:, :CAP, :] = jnp.broadcast_to(packed[None], (devices, CAP, BLK))
+        packet_ref[:, first : first + 8, :] = jnp.broadcast_to(piece[None], (copies_out, 8, BLK))
+    packet_ref[:, :CAP, :] = jnp.broadcast_to(packed[None], (copies_out, CAP, BLK))
     for copy in stores:
         copy.wait()
 
@@ -310,7 +317,7 @@
     return jnp.concatenate(total, axis=0)
 
 
-def grads_kernel(where_ref, got_ref, travel_hbm, unit_hbm, rain_hbm, grad_hbm, resp_hbm,
+def grads_kernel(where_ref, own_ref, other_ref, travel_hbm, unit_hbm, rain_hbm, grad_hbm, resp_hbm,
                  send_ref, drive_ref, weight_ref, ids_ref,
                  travel_ref, unit_ref, rain_ref, grad_ref, resp_ref,
                  lateral_ref, fast_ref, slow_ref, padded_ref, sems, *, levels, basins, units_here):
@@ -327,7 +334,11 @@
     )
     devices = levels * basins
     lanes = ids_ref.shape[2]
-    most = jnp.max(got_ref[basins:, CAP : CAP + 8, :], axis=0)[2:3, :]
+    columns = basins // 2
+    core = where_ref[2]
+    most = jnp.max(
+        jnp.maximum(own_ref[columns:, CAP : CAP + 8, :], other_ref[columns:, CAP : CAP + 8, :]), axis=0
+    )[2:3, :]
     ids_ref[0] = jnp.broadcast_to(jnp.max(most, axis=1, keepdims=True), (8, lanes))
     outlets = basins * blocks
     halves = units_here // BLK
@@ -336,16 +347,23 @@
     padded_ref[steps:, :] = jnp.zeros((steps, lanes), F32)
     back = [None]
     for l in range(1, levels):
-        first = l * basins
-        data = got_ref[first : first + basins, :CAP, :].reshape(basins * CAP, BLK)
+        group = slice(l * columns, (l + 1) * columns)
+        data = jnp.concatenate(
+            [ref[group, :CAP, :].reshape(columns * CAP, BLK) for ref in (own_ref, other_ref)], axis=0
+        )
         turned = jnp.transpose(data)
         labels = jnp.concatenate(
             [
-                jnp.sum(got_ref[first : first + basins, CAP + 8 * g : CAP + 8 * g + 8, :], axis=0)
-                for g in range((got_ref.shape[1] - CAP) // 8)
+                jnp.sum(
+                    own_ref[group, CAP + 8 * g : CAP + 8 * g + 8, :]
+                    + other_ref[group, CAP + 8 * g : CAP + 8 * g + 8, :],
+                    axis=0,
+                )
+                for g in range((own_ref.shape[1] - CAP) // 8)
             ],
             axis=1,
         )[:, : basins * CAP]
+        labels = jnp.where(core == 1, pltpu.roll(labels, columns * CAP, 1), labels)
         slot_of = (
             jnp.broadcast_to(labels[0:1], (lanes, basins * CAP))
             == iota((lanes, basins * CAP), 0).astype(F32) + 1.0
@@ -378,9 +396,13 @@
     at = iota((2 * owned, devices * 8), 0)
     kind = at // owned
     inside = at - kind * owned
-    line = inside // halves * 8 + 4 + kind * halves + inside % halves
+    owner = inside // halves
+    line = owner // 2 * 8 + 4 + kind * halves + inside % halves
+    line = line + (owner + core) % 2 * (devices * 4)
     compact = (iota((2 * owned, devices * 8), 1) == line).astype(BF16)
-    table = got_ref[:, CAP : CAP + 8, :].reshape(devices * 8, BLK)
+    table = jnp.concatenate(
+        [ref[:, CAP : CAP + 8, :].reshape(devices * 4, BLK) for ref in (own_ref, other_ref)], axis=0
+    )
     spread = pick(pick_right(compact, table, NN), places, NN)
     row_at = iota((owned, reaches), 0) == jnp.broadcast_to(unit_row, (owned, reaches))
     fast_rate = jnp.sum(jnp.where(row_at, spread[:owned], 0.0), axis=0, keepdims=True)
@@ -550,7 +572,7 @@
     _, steps, reaches = runoff.shape
     blocks = reaches // BLK
     levels = lax.axis_size("level")
-    basins = lax.axis_size("basin")
+    basins = lax.axis_size("column") * lax.axis_size("core")
     devices = levels * basins
     outlets = basins * blocks
     lanes = -(-outlets // BLK) * BLK
@@ -569,11 +591,13 @@
     answers = pltpu.VMEM((blocks, steps, BLK), F32)
     moves_shape = (count + 1, 2, blocks, BLK, BLK)
     height = CAP + 8 * (-(-basins * CAP // BLK))
-    where = jnp.stack([lax.axis_index("level"), lax.axis_index("basin")]).astype(jnp.int32)
+    where = jnp.stack(
+        [lax.axis_index("level"), lax.axis_index(BASIN_AXES), lax.axis_index("core")]
+    ).astype(jnp.int32)
     packet, grad, resp, moves = pl.pallas_call(
         lambda *refs: blocks_kernel(*refs, basins=basins),
         out_shape=(
-            shape((devices, height, BLK), F32),
+            shape((devices // 2, height, BLK), F32),
             shape((steps, reaches), F32),
             shape((blocks, steps, BLK), F32),
             shape(moves_shape, BF16),
@@ -588,7 +612,7 @@
         compiler_params=params,
         name="blocks",
     )(where, *still(travel, downstream, inflow_src, rates, cotangent))
-    got = lax.all_to_all(packet, LEVELS_AXES, 0, 0)
+    got = exchange(packet)
 
     def finish(got):
         sent, drive, weights, numbers = pl.pallas_call(
@@ -599,13 +623,13 @@
                 shape((levels, steps, lanes), F32),
                 shape((levels, 8, lanes), F32),
             ),
-            in_specs=[smem, vmem] + [hbm] * 5,
+            in_specs=[smem, vmem, vmem] + [hbm] * 5,
             out_specs=(vmem,) * 4,
             scratch_shapes=[row_f32, row_i32, stack, series, answers, stack, stack, stack,
                             pltpu.VMEM((2 * steps, lanes), F32), pltpu.SemaphoreType.DMA((blocks + 4,))],
             compiler_params=params,
             name="grads",
-        )(where, got, *still(travel, reach_unit, runoff, grad, resp))
+        )(where, *got, *still(travel, reach_unit, runoff, grad, resp))
         swapped = lax.all_to_all(sent, LEVELS_AXES, 0, 0)
         *near_moves, coefs, source, full = pl.pallas_call(
             fetch_kernel,
@@ -640,11 +664,16 @@
     flows, totals, full = finish(got)
     flows, totals = lax.cond(
         full > CAP,
-        lambda done: finish(spread_sources(got.shape, grad, resp, travel, inflow_src, rates))[:2],
+        lambda done: finish(spread_sources(packet.shape, grad, resp, travel, inflow_src, rates))[:2],
         lambda done: done,
         (flows, totals),
     )
     return flows, totals
+
+
+def exchange(packet):
+    own = lax.all_to_all(packet, ("level", "column"), 0, 0)
+    return own, lax.ppermute(own, "core", [(0, 1), (1, 0)])
 
 
 def spread_sources(packet_shape, grad, resp, travel, inflow_src, rates):
@@ -658,8 +687,8 @@
         name="relay",
     )(*still(*values))
     blocks, steps, _ = resp.shape
-    basins = lax.axis_size("basin")
-    basin_id = lax.axis_index("basin")
+    basins = lax.axis_size("column") * lax.axis_size("core")
+    basin_id = lax.axis_index(BASIN_AXES)
     outlets = basins * blocks
     reaches = blocks * BLK
     coef_in, coef_prev, _ = coefficients(travel)
@@ -671,9 +700,9 @@
     table = jnp.concatenate([back, ahead, jnp.broadcast_to(block_of[None], (BLK, reaches))], axis=0)
     chosen = (inflow_src == jnp.arange(outlets)[:, None]).astype(F32)
     mine = lax.dot_general(chosen, table, NT, precision=lax.Precision.HIGHEST)
-    parts = lax.all_to_all(mine.reshape(basins, blocks, 2 * steps + BLK), "basin", 0, 0).sum(axis=0)
+    parts = lax.all_to_all(mine.reshape(basins, blocks, 2 * steps + BLK), BASIN_AXES, 0, 0).sum(axis=0)
     width = (packet_shape[1] - CAP) // 8 * BLK
-    place = jnp.arange(blocks) + basin_id * CAP
+    place = jnp.arange(blocks) + label_lane(basin_id, basins)
     onto = (jnp.arange(width)[None, :] == place[:, None]).astype(F32)
     slot_row = ((jnp.arange(blocks) + basin_id * blocks + 1).astype(F32)[:, None] * onto).sum(axis=0)
     block_row = (parts[:, 2 * steps : 2 * steps + 1] * onto).sum(axis=0)
@@ -686,23 +715,20 @@
     packet = jnp.concatenate(
         [parts[:, : 2 * steps], jnp.zeros((CAP - blocks, 2 * steps), F32), labels], axis=0
     )
-    return lax.all_to_all(jnp.broadcast_to(packet[None], packet_shape), LEVELS_AXES, 0, 0)
+    return exchange(jnp.broadcast_to(packet[None], packet_shape))
 
 
 def solution(mesh):
-    placed = (
-        P("level", None, "basin"),
-        P("level", "basin"),
-        P("level", "basin"),
-        P("level", "basin"),
-        P("level", "basin"),
-        P(None, ("level", "basin")),
-        P("level", None, "basin"),
-    )
+    fine = jax.sharding.Mesh(
+        mesh.devices.reshape(mesh.shape["level"], -1, 2), ("level", "column", "core")
+    )
+    series = P("level", None, BASIN_AXES)
+    row = P("level", BASIN_AXES)
+    units = P(None, LEVELS_AXES)
     return jax.shard_map(
         per_device,
-        mesh=mesh,
-        in_specs=placed,
-        out_specs=(P("level", None, "basin"), P(None, ("level", "basin"))),
+        mesh=fine,
+        in_specs=(series, row, row, row, row, units, series),
+        out_specs=(series, units),
         check_vma=False,
     )

time: 50.1 us -> 48.1 us (0.960)
  blocking collectives: 20.6 us -> 17.3 us
  waiting for transfers between devices: 5.23 us -> 6.67 us
    all_to_all x1, blocking collectives: 20.6 us -> 17.3 us  [exchange(): own = lax.all_to_all(packet, ('level', 'column'), 0, 0)]
    ppermute x0 -> x1, waiting for transfers between devices: none -> 1.44 us  [exchange(): return (own, lax.ppermute(own, 'core', [(0, 1), (1, 0)]))]
  transfers between devices with their start and end apart: 1 -> 2, of which waited for: 1 -> 2; matrix products, arithmetic and copies ran while one was open for 0% -> 0% of each run, Pallas kernels for 5% -> 5%
where the time goes in v4:
time: 48.1 us; the launch traced here: 47.7 us
  Pallas kernels  19.4 us (40%)
  blocking collectives  17.3 us (36%)
  waiting for transfers between devices  6.67 us (14%)
  starting transfers between devices  2.6 us (5%)
  between operations  1.51 us (3%)
    all_to_all x1, blocking collectives, exchange(): own = lax.all_to_all(packet, ('level', 'column'), 0, 0)  17.3 us
    pallas_call x1, Pallas kernels, per_device(): pl.pallas_call(lambda *refs: blocks_kernel(*refs, basins=basins), out_sha...  7.71 us
    pallas_call x1, Pallas kernels, finish(): pl.pallas_call(lambda *refs: grads_kernel(*refs, levels=levels, basins=ba...  5.26 us
    all_to_all x1, waiting for transfers between devices, finish(): swapped = lax.all_to_all(sent, LEVELS_AXES, 0, 0)  5.23 us
    pallas_call x1, Pallas kernels, finish(): pl.pallas_call(lambda *refs: flows_kernel(*refs, levels=levels, basins=ba...  4.15 us
    all_to_all x1, starting transfers between devices, finish(): swapped = lax.all_to_all(sent, LEVELS_AXES, 0, 0)  2.59 us
    pallas_call x1, Pallas kernels, finish(): pl.pallas_call(fetch_kernel, out_shape=(*[shape(moves_shape[1:], BF16)] *...  2.29 us
    ppermute x1, waiting for transfers between devices, exchange(): return (own, lax.ppermute(own, 'core', [(0, 1), (1, 0)]))  1.44 us
  transfers between devices with their start and end apart: 2, of which 2 were waited for; matrix products, arithmetic and copies ran while one was open for 0% of the time, Pallas kernels for 5%

profile of v4, /device:TPU:0, one launch (start us, length us, event | category | flops | bytes accessed | tf_op | source)
XLA Modules:
  0.0 47.7 jit_solution(9536241621828452768)
XLA Ops:
  0.6 0.1 pad_add_fusion.refs_0_
  0.7 7.7 %blocks.1 = (f32[16,24,128]{2,1,0:T(8,128)S(1)}, f32[64,1024]{1,0:T(8,128)}, f32[8,64,128]{2,1,0:T(8,128)}, bf16[7,2,8,128,128]{4,3,2,1,0:T(8,128)(2,1)}) custom-call(s32[3]{0:T(128)S(1)} %pad_add_fusion.refs_0_, f32[1,1024]{1,0:T(1,128)} %travel_hbm.1, s32[1,1024]{1,0:T(1,128)} %refs_2_.1, s32[1,1024]{1,0:T(1,128)} %src_hbm.1, f32[2,256]{1,0:T(2,128)} %refs_4_.2, ...), custom_call_target="tpu_custom_call" | custom-call | tf_op jit(solution)/shard_map/blocks/pallas_call | solution.py:597
  8.4 17.3 %all_to_all.23.refs_1_ = f32[16,24,128]{2,1,0:T(8,128)S(1)} all-to-all(f32[16,24,128]{2,1,0:T(8,128)S(1)} %get-tuple-element.77), channel_id=1, replica_groups=mesh['level'=4,'column'=4,'core'=2] {'level','column'}, dimensions={0} | all-to-all | bytes 393216 | tf_op jit(solution)/shard_map/all_to_all | solution.py:675
  25.7 0.0 collective-permute-start.1
  25.7 1.4 %collective-permute-done.1.refs_2_ = f32[16,24,128]{2,1,0:T(8,128)S(1)} collective-permute-done((f32[16,24,128]{2,1,0:T(8,128)S(1)}, f32[16,24,128]{2,1,0:T(8,128)S(1)}, u32[]{:S(2)}, u32[]{:S(2)}) %collective-permute-start.1) | collective-permute-done | bytes 196640 | tf_op jit(solution)/shard_map/ppermute | solution.py:676
  27.1 5.3 %grads.3 = (f32[32,8,128]{2,1,0:T(8,128)}, f32[8,64,128]{2,1,0:T(8,128)S(1)}, f32[4,64,128]{2,1,0:T(8,128)S(1)}, f32[4,8,128]{2,1,0:T(8,128)S(1)}) custom-call(s32[3]{0:T(128)S(1)} %pad_add_fusion.refs_0_, f32[16,24,128]{2,1,0:T(8,128)S(1)} %all_to_all.23.refs_1_, f32[16,24,128]{2,1,0:T(8,128)S(1)} %collective-permute-done.1.refs_2_, f32[1,1024]{1,0:T(1,128)} %travel_hbm.1, ...), custom_call_target="tpu_custom_call" | custom-call | tf_op jit(solution)/shard_map/grads/pallas_call | solution.py:618
  32.4 2.6 %all-to-all-start.4 = ((f32[32,8,128]{2,1,0:T(8,128)}), f32[32,8,128]{2,1,0:T(8,128)S(1)}, u32[]{:S(2)}, u32[]{:S(2)}) async-start(f32[32,8,128]{2,1,0:T(8,128)} %get-tuple-element.83), calls=%async_computation.4 | async-start | bytes 262144 | tf_op jit(solution)/shard_map/all_to_all | solution.py:633
  35.0 2.3 %fetch.3 = (bf16[2,8,128,128]{3,2,1,0:T(8,128)(2,1)S(1)}, bf16[2,8,128,128]{3,2,1,0:T(8,128)(2,1)S(1)}, bf16[2,8,128,128]{3,2,1,0:T(8,128)(2,1)S(1)}, bf16[2,8,1...) custom-call(f32[4,8,128]{2,1,0:T(8,128)S(1)} %get-tuple-element.80.i, ...), custom_call_target="tpu_custom_call" | custom-call | tf_op jit(solution)/shard_map/fetch/pallas_call | solution.py:634
  37.9 5.2 %all-to-all-done.4.refs_1_ = f32[32,8,128]{2,1,0:T(8,128)S(1)} async-done(((f32[32,8,128]{2,1,0:T(8,128)}), f32[32,8,128]{2,1,0:T(8,128)S(1)}, u32[]{:S(2)}, u32[]{:S(2)}) %all-to-all-start.4) | async-done | bytes 131104 | tf_op jit(solution)/shard_map/all_to_all | solution.py:633
  43.2 4.2 %flows.3 = (f32[1,64,1024]{2,1,0:T(8,128)}, f32[2,256]{1,0:T(2,128)}) custom-call(s32[3]{0:T(128)S(1)} %pad_add_fusion.refs_0_, f32[32,8,128]{2,1,0:T(8,128)S(1)} %all-to-all-done.4.refs_1_, f32[2,1024]{1,0:T(2,128)S(1)} %get-tuple-element.84.refs_2_, bf16[128,1024]{1,0:T(8,128)(2,1)S(1)} %get-tuple-element.85.refs_3_, ...), custom_call_target="tpu_custom_call" | custom-call | tf_op jit(solution)/shard_map/flows/pallas_call | solution.py:649
  47.3 0.2 conditional.1
Async XLA Ops:
  25.7 1.4 %collective-permute-start.1 = (f32[16,24,128]{2,1,0:T(8,128)S(1)}, f32[16,24,128]{2,1,0:T(8,128)S(1)}, u32[]{:S(2)}, u32[]{:S(2)}) collective-permute-start(f32[16,24,128]{2,1,0:T(8,128)S(1)} %all_to_all.23.refs_1_), channel_id=1, source_target_pairs={{0,1},{1,0},{2,3},{3,2},{4,5},{5,4},{6,7},{7,6},{8,9},{9,8},{10,11... | collective-permute-start | bytes 589832 | tf_op jit(solution)/shard_map/ppermute | solution.py:676
  32.4 10.8 %all-to-all-start.4 = ((f32[32,8,128]{2,1,0:T(8,128)}), f32[32,8,128]{2,1,0:T(8,128)S(1)}, u32[]{:S(2)}, u32[]{:S(2)}) async-start(f32[32,8,128]{2,1,0:T(8,128)} %get-tuple-element.83), calls=%async_computation.4 | async-start | bytes 262144 | tf_op jit(solution)/shard_map/all_to_all | solution.py:633

commit v5 on v4

--- a/solution.py
+++ b/solution.py
@@ -189,7 +189,10 @@
                 scale = jnp.sum(power[b], axis=1, keepdims=True)
                 product = scale * pick_right(hops[b], joined, NN)
             else:
-                product = mm(power[b].astype(BF16), joined.astype(BF16), NN)
+                filled = BLK - (1 << (level - 1))
+                product = mm(power[b][:filled].astype(BF16), joined.astype(BF16), NN)
+                empty = jnp.zeros((BLK - filled, joined.shape[1]), F32)
+                product = jnp.concatenate([product, empty], axis=0)
             if level <= 2:
                 hops[b] = mm(hops[b], hops[b], NN).astype(BF16)
             if level == 1:
@@ -515,7 +518,6 @@
             at = 4 + k * parts + h
             rate_ref[k : k + 1, h * BLK : (h + 1) * BLK] = summed[at : at + 1]
     stores = [pltpu.make_async_copy(rate_ref, rate_hbm, out_sems.at[blocks])]
-    stores[0].start()
     padded_ref[:steps, :] = jnp.zeros((steps, lanes), F32)
     rows = basins * 8
     row = iota((rows, lanes), 0)
@@ -564,6 +566,7 @@
         copy = pltpu.make_async_copy(flow_ref.at[:, side], flow_hbm.at[0, :, side], out_sems.at[b])
         copy.start()
         stores.append(copy)
+    stores[0].start()
     for copy in stores:
         copy.wait()
 

time: 48.1 us -> 47.7 us (level)
  no operation moved by 1% of the time
where the time goes in v5:
time: 47.7 us; the launch traced here: 47.4 us
  Pallas kernels  19.1 us (40%)
  blocking collectives  17.3 us (36%)
  waiting for transfers between devices  6.67 us (14%)
  starting transfers between devices  2.6 us (5%)
  between operations  1.51 us (3%)
    all_to_all x1, blocking collectives, exchange(): own = lax.all_to_all(packet, ('level', 'column'), 0, 0)  17.3 us
    pallas_call x1, Pallas kernels, per_device(): pl.pallas_call(lambda *refs: blocks_kernel(*refs, basins=basins), out_sha...  7.67 us
    pallas_call x1, Pallas kernels, finish(): pl.pallas_call(lambda *refs: grads_kernel(*refs, levels=levels, basins=ba...  5.26 us
    all_to_all x1, waiting for transfers between devices, finish(): swapped = lax.all_to_all(sent, LEVELS_AXES, 0, 0)  5.23 us
    pallas_call x1, Pallas kernels, finish(): pl.pallas_call(lambda *refs: flows_kernel(*refs, levels=levels, basins=ba...  3.84 us
    all_to_all x1, starting transfers between devices, finish(): swapped = lax.all_to_all(sent, LEVELS_AXES, 0, 0)  2.59 us
    pallas_call x1, Pallas kernels, finish(): pl.pallas_call(fetch_kernel, out_shape=(*[shape(moves_shape[1:], BF16)] *...  2.29 us
    ppermute x1, waiting for transfers between devices, exchange(): return (own, lax.ppermute(own, 'core', [(0, 1), (1, 0)]))  1.44 us
  transfers between devices with their start and end apart: 2, of which 2 were waited for; matrix products, arithmetic and copies ran while one was open for 0% of the time, Pallas kernels for 5%

profile of v5, /device:TPU:0, one launch (start us, length us, event | category | flops | bytes accessed | tf_op | source)
XLA Modules:
  0.0 47.4 jit_solution(6416249142430114626)
XLA Ops:
  0.6 0.1 pad_add_fusion.refs_0_
  0.7 7.7 %blocks.1 = (f32[16,24,128]{2,1,0:T(8,128)S(1)}, f32[64,1024]{1,0:T(8,128)}, f32[8,64,128]{2,1,0:T(8,128)}, bf16[7,2,8,128,128]{4,3,2,1,0:T(8,128)(2,1)}) custom-call(s32[3]{0:T(128)S(1)} %pad_add_fusion.refs_0_, f32[1,1024]{1,0:T(1,128)} %travel_hbm.1, s32[1,1024]{1,0:T(1,128)} %refs_2_.1, s32[1,1024]{1,0:T(1,128)} %src_hbm.1, f32[2,256]{1,0:T(2,128)} %refs_4_.2, ...), custom_call_target="tpu_custom_call" | custom-call | tf_op jit(solution)/shard_map/blocks/pallas_call | solution.py:600
  8.4 17.3 %all_to_all.23.refs_1_ = f32[16,24,128]{2,1,0:T(8,128)S(1)} all-to-all(f32[16,24,128]{2,1,0:T(8,128)S(1)} %get-tuple-element.77), channel_id=1, replica_groups=mesh['level'=4,'column'=4,'core'=2] {'level','column'}, dimensions={0} | all-to-all | bytes 393216 | tf_op jit(solution)/shard_map/all_to_all | solution.py:678
  25.7 0.0 collective-permute-start.1
  25.7 1.4 %collective-permute-done.1.refs_2_ = f32[16,24,128]{2,1,0:T(8,128)S(1)} collective-permute-done((f32[16,24,128]{2,1,0:T(8,128)S(1)}, f32[16,24,128]{2,1,0:T(8,128)S(1)}, u32[]{:S(2)}, u32[]{:S(2)}) %collective-permute-start.1) | collective-permute-done | bytes 196640 | tf_op jit(solution)/shard_map/ppermute | solution.py:679
  27.1 5.3 %grads.3 = (f32[32,8,128]{2,1,0:T(8,128)}, f32[8,64,128]{2,1,0:T(8,128)S(1)}, f32[4,64,128]{2,1,0:T(8,128)S(1)}, f32[4,8,128]{2,1,0:T(8,128)S(1)}) custom-call(s32[3]{0:T(128)S(1)} %pad_add_fusion.refs_0_, f32[16,24,128]{2,1,0:T(8,128)S(1)} %all_to_all.23.refs_1_, f32[16,24,128]{2,1,0:T(8,128)S(1)} %collective-permute-done.1.refs_2_, f32[1,1024]{1,0:T(1,128)} %travel_hbm.1, ...), custom_call_target="tpu_custom_call" | custom-call | tf_op jit(solution)/shard_map/grads/pallas_call | solution.py:621
  32.4 2.6 %all-to-all-start.4 = ((f32[32,8,128]{2,1,0:T(8,128)}), f32[32,8,128]{2,1,0:T(8,128)S(1)}, u32[]{:S(2)}, u32[]{:S(2)}) async-start(f32[32,8,128]{2,1,0:T(8,128)} %get-tuple-element.83), calls=%async_computation.4 | async-start | bytes 262144 | tf_op jit(solution)/shard_map/all_to_all | solution.py:636
  35.0 2.3 %fetch.3 = (bf16[2,8,128,128]{3,2,1,0:T(8,128)(2,1)S(1)}, bf16[2,8,128,128]{3,2,1,0:T(8,128)(2,1)S(1)}, bf16[2,8,128,128]{3,2,1,0:T(8,128)(2,1)S(1)}, bf16[2,8,1...) custom-call(f32[4,8,128]{2,1,0:T(8,128)S(1)} %get-tuple-element.80.i, ...), custom_call_target="tpu_custom_call" | custom-call | tf_op jit(solution)/shard_map/fetch/pallas_call | solution.py:637
  37.9 5.2 %all-to-all-done.4.refs_1_ = f32[32,8,128]{2,1,0:T(8,128)S(1)} async-done(((f32[32,8,128]{2,1,0:T(8,128)}), f32[32,8,128]{2,1,0:T(8,128)S(1)}, u32[]{:S(2)}, u32[]{:S(2)}) %all-to-all-start.4) | async-done | bytes 131104 | tf_op jit(solution)/shard_map/all_to_all | solution.py:636
  43.2 3.8 %flows.3 = (f32[1,64,1024]{2,1,0:T(8,128)}, f32[2,256]{1,0:T(2,128)}) custom-call(s32[3]{0:T(128)S(1)} %pad_add_fusion.refs_0_, f32[32,8,128]{2,1,0:T(8,128)S(1)} %all-to-all-done.4.refs_1_, f32[2,1024]{1,0:T(2,128)S(1)} %get-tuple-element.84.refs_2_, bf16[128,1024]{1,0:T(8,128)(2,1)S(1)} %get-tuple-element.85.refs_3_, ...), custom_call_target="tpu_custom_call" | custom-call | tf_op jit(solution)/shard_map/flows/pallas_call | solution.py:652
  47.0 0.2 conditional.1
Async XLA Ops:
  25.7 1.4 %collective-permute-start.1 = (f32[16,24,128]{2,1,0:T(8,128)S(1)}, f32[16,24,128]{2,1,0:T(8,128)S(1)}, u32[]{:S(2)}, u32[]{:S(2)}) collective-permute-start(f32[16,24,128]{2,1,0:T(8,128)S(1)} %all_to_all.23.refs_1_), channel_id=1, source_target_pairs={{0,1},{1,0},{2,3},{3,2},{4,5},{5,4},{6,7},{7,6},{8,9},{9,8},{10,11... | collective-permute-start | bytes 589832 | tf_op jit(solution)/shard_map/ppermute | solution.py:679
  32.4 10.8 %all-to-all-start.4 = ((f32[32,8,128]{2,1,0:T(8,128)}), f32[32,8,128]{2,1,0:T(8,128)S(1)}, u32[]{:S(2)}, u32[]{:S(2)}) async-start(f32[32,8,128]{2,1,0:T(8,128)} %get-tuple-element.83), calls=%async_computation.4 | async-start | bytes 262144 | tf_op jit(solution)/shard_map/all_to_all | solution.py:636

commit v6 on v5

--- a/solution.py
+++ b/solution.py
@@ -342,7 +342,7 @@
     most = jnp.max(
         jnp.maximum(own_ref[columns:, CAP : CAP + 8, :], other_ref[columns:, CAP : CAP + 8, :]), axis=0
     )[2:3, :]
-    ids_ref[0] = jnp.broadcast_to(jnp.max(most, axis=1, keepdims=True), (8, lanes))
+    ids_ref[0] = jnp.broadcast_to(jnp.concatenate([most] * (lanes // BLK), axis=1), (8, lanes))
     outlets = basins * blocks
     halves = units_here // BLK
     level_id = where_ref[0]

time: 47.7 us -> 47.7 us (level)
  no operation moved by 1% of the time
where the time goes in v6:
time: 47.7 us; the launch traced here: 47.4 us
  Pallas kernels  19.1 us (40%)
  blocking collectives  17.3 us (36%)
  waiting for transfers between devices  6.67 us (14%)
  starting transfers between devices  2.6 us (5%)
  between operations  1.51 us (3%)
    all_to_all x1, blocking collectives, exchange(): own = lax.all_to_all(packet, ('level', 'column'), 0, 0)  17.3 us
    pallas_call x1, Pallas kernels, per_device(): pl.pallas_call(lambda *refs: blocks_kernel(*refs, basins=basins), out_sha...  7.67 us
    pallas_call x1, Pallas kernels, finish(): pl.pallas_call(lambda *refs: grads_kernel(*refs, levels=levels, basins=ba...  5.26 us
    all_to_all x1, waiting for transfers between devices, finish(): swapped = lax.all_to_all(sent, LEVELS_AXES, 0, 0)  5.23 us
    pallas_call x1, Pallas kernels, finish(): pl.pallas_call(lambda *refs: flows_kernel(*refs, levels=levels, basins=ba...  3.84 us
    all_to_all x1, starting transfers between devices, finish(): swapped = lax.all_to_all(sent, LEVELS_AXES, 0, 0)  2.59 us
    pallas_call x1, Pallas kernels, finish(): pl.pallas_call(fetch_kernel, out_shape=(*[shape(moves_shape[1:], BF16)] *...  2.29 us
    ppermute x1, waiting for transfers between devices, exchange(): return (own, lax.ppermute(own, 'core', [(0, 1), (1, 0)]))  1.44 us
  transfers between devices with their start and end apart: 2, of which 2 were waited for; matrix products, arithmetic and copies ran while one was open for 0% of the time, Pallas kernels for 5%

profile of v6, /device:TPU:0, one launch (start us, length us, event | category | flops | bytes accessed | tf_op | source)
XLA Modules:
  0.0 47.4 jit_solution(13823716539649985138)
XLA Ops:
  0.6 0.1 pad_add_fusion.refs_0_
  0.7 7.7 %blocks.1 = (f32[16,24,128]{2,1,0:T(8,128)S(1)}, f32[64,1024]{1,0:T(8,128)}, f32[8,64,128]{2,1,0:T(8,128)}, bf16[7,2,8,128,128]{4,3,2,1,0:T(8,128)(2,1)}) custom-call(s32[3]{0:T(128)S(1)} %pad_add_fusion.refs_0_, f32[1,1024]{1,0:T(1,128)} %travel_hbm.1, s32[1,1024]{1,0:T(1,128)} %refs_2_.1, s32[1,1024]{1,0:T(1,128)} %src_hbm.1, f32[2,256]{1,0:T(2,128)} %refs_4_.2, ...), custom_call_target="tpu_custom_call" | custom-call | tf_op jit(solution)/shard_map/blocks/pallas_call | solution.py:600
  8.4 17.3 %all_to_all.23.refs_1_ = f32[16,24,128]{2,1,0:T(8,128)S(1)} all-to-all(f32[16,24,128]{2,1,0:T(8,128)S(1)} %get-tuple-element.77), channel_id=1, replica_groups=mesh['level'=4,'column'=4,'core'=2] {'level','column'}, dimensions={0} | all-to-all | bytes 393216 | tf_op jit(solution)/shard_map/all_to_all | solution.py:678
  25.7 0.0 collective-permute-start.1
  25.7 1.4 %collective-permute-done.1.refs_2_ = f32[16,24,128]{2,1,0:T(8,128)S(1)} collective-permute-done((f32[16,24,128]{2,1,0:T(8,128)S(1)}, f32[16,24,128]{2,1,0:T(8,128)S(1)}, u32[]{:S(2)}, u32[]{:S(2)}) %collective-permute-start.1) | collective-permute-done | bytes 196640 | tf_op jit(solution)/shard_map/ppermute | solution.py:679
  27.1 5.3 %grads.3 = (f32[32,8,128]{2,1,0:T(8,128)}, f32[8,64,128]{2,1,0:T(8,128)S(1)}, f32[4,64,128]{2,1,0:T(8,128)S(1)}, f32[4,8,128]{2,1,0:T(8,128)S(1)}) custom-call(s32[3]{0:T(128)S(1)} %pad_add_fusion.refs_0_, f32[16,24,128]{2,1,0:T(8,128)S(1)} %all_to_all.23.refs_1_, f32[16,24,128]{2,1,0:T(8,128)S(1)} %collective-permute-done.1.refs_2_, f32[1,1024]{1,0:T(1,128)} %travel_hbm.1, ...), custom_call_target="tpu_custom_call" | custom-call | tf_op jit(solution)/shard_map/grads/pallas_call | solution.py:621
  32.4 2.6 %all-to-all-start.4 = ((f32[32,8,128]{2,1,0:T(8,128)}), f32[32,8,128]{2,1,0:T(8,128)S(1)}, u32[]{:S(2)}, u32[]{:S(2)}) async-start(f32[32,8,128]{2,1,0:T(8,128)} %get-tuple-element.83), calls=%async_computation.4 | async-start | bytes 262144 | tf_op jit(solution)/shard_map/all_to_all | solution.py:636
  35.0 2.3 %fetch.3 = (bf16[2,8,128,128]{3,2,1,0:T(8,128)(2,1)S(1)}, bf16[2,8,128,128]{3,2,1,0:T(8,128)(2,1)S(1)}, bf16[2,8,128,128]{3,2,1,0:T(8,128)(2,1)S(1)}, bf16[2,8,1...) custom-call(f32[4,8,128]{2,1,0:T(8,128)S(1)} %get-tuple-element.80.i, ...), custom_call_target="tpu_custom_call" | custom-call | tf_op jit(solution)/shard_map/fetch/pallas_call | solution.py:637
  37.9 5.2 %all-to-all-done.4.refs_1_ = f32[32,8,128]{2,1,0:T(8,128)S(1)} async-done(((f32[32,8,128]{2,1,0:T(8,128)}), f32[32,8,128]{2,1,0:T(8,128)S(1)}, u32[]{:S(2)}, u32[]{:S(2)}) %all-to-all-start.4) | async-done | bytes 131104 | tf_op jit(solution)/shard_map/all_to_all | solution.py:636
  43.2 3.8 %flows.3 = (f32[1,64,1024]{2,1,0:T(8,128)}, f32[2,256]{1,0:T(2,128)}) custom-call(s32[3]{0:T(128)S(1)} %pad_add_fusion.refs_0_, f32[32,8,128]{2,1,0:T(8,128)S(1)} %all-to-all-done.4.refs_1_, f32[2,1024]{1,0:T(2,128)S(1)} %get-tuple-element.84.refs_2_, bf16[128,1024]{1,0:T(8,128)(2,1)S(1)} %get-tuple-element.85.refs_3_, ...), custom_call_target="tpu_custom_call" | custom-call | tf_op jit(solution)/shard_map/flows/pallas_call | solution.py:652
  47.0 0.2 conditional.1
Async XLA Ops:
  25.7 1.4 %collective-permute-start.1 = (f32[16,24,128]{2,1,0:T(8,128)S(1)}, f32[16,24,128]{2,1,0:T(8,128)S(1)}, u32[]{:S(2)}, u32[]{:S(2)}) collective-permute-start(f32[16,24,128]{2,1,0:T(8,128)S(1)} %all_to_all.23.refs_1_), channel_id=1, source_target_pairs={{0,1},{1,0},{2,3},{3,2},{4,5},{5,4},{6,7},{7,6},{8,9},{9,8},{10,11... | collective-permute-start | bytes 589832 | tf_op jit(solution)/shard_map/ppermute | solution.py:679
  32.4 10.8 %all-to-all-start.4 = ((f32[32,8,128]{2,1,0:T(8,128)}), f32[32,8,128]{2,1,0:T(8,128)S(1)}, u32[]{:S(2)}, u32[]{:S(2)}) async-start(f32[32,8,128]{2,1,0:T(8,128)} %get-tuple-element.83), calls=%async_computation.4 | async-start | bytes 262144 | tf_op jit(solution)/shard_map/all_to_all | solution.py:636
